TPU v7x, 32 devices: a whole 2x2x4 slice. The times are simulated.
32 devices in a mesh: dp: 8 (over z, y), frame: 4 (over x, core).
Axes of the slice: x: 2, y: 2, z: 4, core: 2. Of those that a mesh axis runs over, the one named last changes fastest.
Arguments:
- mel_frames: bfloat16 [16, 3008, 80], P('dp', 'frame'), may hold values from -6 to 6
- window_count: int32 [8], P('dp'), may hold values from 1 to 2, as said below
- stem_weight: bfloat16 [3, 80, 512], replicated, may hold values from -0.375 to 0.375
- stem_bias: float32 [512], replicated, may hold values from -1.5 to 1.5
- reduce_weight: bfloat16 [3, 512, 512], replicated, may hold values from -0.15625 to 0.15625
- reduce_bias: float32 [512], replicated, may hold values from -1.5 to 1.5
- first_gain: float32 [512], replicated, may hold values from 0.5 to 1.5
- first_shift: float32 [512], replicated, may hold values from -1.5 to 1.5
- query_weight: bfloat16 [512, 512], replicated, may hold values from -0.25 to 0.25
- query_bias: float32 [512], replicated, may hold values from -1.5 to 1.5
- key_weight: bfloat16 [512, 512], replicated, may hold values from -0.25 to 0.25
- value_weight: bfloat16 [512, 512], replicated, may hold values from -0.25 to 0.25
- value_bias: float32 [512], replicated, may hold values from -1.5 to 1.5
- output_weight: bfloat16 [512, 512], replicated, may hold values from -4 to 4
- output_bias: float32 [512], replicated, may hold values from -1.5 to 1.5
- second_gain: float32 [512], replicated, may hold values from 0.5 to 1.5
- second_shift: float32 [512], replicated, may hold values from -1.5 to 1.5
- hidden_weight: bfloat16 [512, 2048], replicated, may hold values from -0.25 to 0.25
- hidden_bias: float32 [2048], replicated, may hold values from -1.5 to 1.5
- return_weight: bfloat16 [2048, 512], replicated, may hold values from -0.125 to 0.125
- return_bias: float32 [512], replicated, may hold values from -1.5 to 1.5
- cotangent: bfloat16 [16, 1504, 512], P('dp', 'frame'), may hold values from -6 to 6
Outputs:
- layer_output: bfloat16 [16, 1504, 512], P('dp', 'frame')
- mel_gradient: float32 [16, 3008, 80], P('dp', 'frame')
- stem_weight_gradient: float32 [3, 80, 512], replicated
- stem_bias_gradient: float32 [512], replicated
- reduce_weight_gradient: float32 [3, 512, 512], replicated
- reduce_bias_gradient: float32 [512], replicated
- first_gain_gradient: float32 [512], replicated
- first_shift_gradient: float32 [512], replicated
- query_weight_gradient: float32 [512, 512], replicated
- query_bias_gradient: float32 [512], replicated
- key_weight_gradient: float32 [512, 512], replicated
- value_weight_gradient: float32 [512, 512], replicated
- value_bias_gradient: float32 [512], replicated
- output_weight_gradient: float32 [512, 512], replicated
- output_bias_gradient: float32 [512], replicated
- second_gain_gradient: float32 [512], replicated
- second_shift_gradient: float32 [512], replicated
- hidden_weight_gradient: float32 [512, 2048], replicated
- hidden_bias_gradient: float32 [2048], replicated
- return_weight_gradient: float32 [2048, 512], replicated
- return_bias_gradient: float32 [512], replicated
Inputs may be any that keep to these rules, and one draw needn't show every extreme that they name: `window_count`: slots of a data group at or beyond its count hold no window. Some group has exactly 2 windows and some group exactly 1.
All inputs are finite; a program needn't handle non-finite values.
Results may differ from a plain program's by a relative error of at most 0.013.
Values may be sent and summed in bfloat16 or wider, within the bound.
A program may use at most 192 MiB of HBM per device.

v0:
```python
import math

import jax
import jax.numpy as jnp
from jax import lax
from jax.sharding import PartitionSpec as P

HEADS = 8


epsilon = 1e-05


def extended_2(cells, sides, width):
    for axis, dim in sides:
        count = lax.axis_size(axis)
        ends = count - 1
        head = lax.slice_in_dim(cells, 0, width, axis=dim)
        tail = lax.slice_in_dim(cells, cells.shape[dim] - width, cells.shape[dim], axis=dim)
        cells = jnp.concatenate(
            [
                lax.ppermute(tail, axis, [(i, (i + 1) % count) for i in range(ends)]),
                cells,
                lax.ppermute(head, axis, [((i + 1) % count, i) for i in range(ends)]),
            ],
            axis=dim,
        )
    return cells


def from_behind(block, axis, distance):
    devices = range(lax.axis_size(axis))
    route = [(i - distance, i) for i in devices if i - distance in devices]
    return lax.ppermute(block, axis, route)


def gelu_exact(argument):
    return jax.nn.gelu(argument, approximate=False)


def layer_norm(argument, norm_gain, norm_shift):
    centred = argument - jnp.mean(argument, axis=-1, keepdims=True)
    variance = jnp.mean(centred * centred, axis=-1, keepdims=True)
    return centred * lax.rsqrt(variance + epsilon) * norm_gain + norm_shift


def sinusoid(start_token, length, model_width):
    halfway = model_width // 2
    increment = math.log(10000.0) / (halfway - 1)
    inverse = jnp.exp(-increment * jnp.arange(halfway, dtype=jnp.float32))
    places = (start_token + jnp.arange(length, dtype=jnp.int32)).astype(jnp.float32)
    angles = places[:, None] * inverse[None, :]
    return jnp.concatenate([jnp.sin(angles), jnp.cos(angles)], axis=1)


def times_matrix(left, right):
    return jnp.dot(left, right, preferred_element_type=jnp.float32)


def outer_total(left, right):
    return lax.dot_general(
        left, right, (((0,), (0,)), ((), ())), preferred_element_type=jnp.float32
    )


def times_transpose(left, right):
    return lax.dot_general(
        left, right, (((1,), (1,)), ((), ())), preferred_element_type=jnp.float32
    )


def gelu_pull(primal, incoming):
    return jax.vjp(gelu_exact, primal)[1](incoming)[0]


def norm_pull(primal, norm_gain, norm_shift, incoming):
    return jax.vjp(layer_norm, primal, norm_gain, norm_shift)[1](incoming)


def column_total(gradient):
    return jnp.sum(gradient.astype(jnp.float32), axis=0)


def on_device(
    mel_frames,
    window_count,
    stem_weight,
    stem_bias,
    reduce_weight,
    reduce_bias,
    first_gain,
    first_shift,
    query_weight,
    query_bias,
    key_weight,
    value_weight,
    value_bias,
    output_weight,
    output_bias,
    second_gain,
    second_shift,
    hidden_weight,
    hidden_bias,
    return_weight,
    return_bias,
    cotangent,
):
    slot_total, frame_rows, mel_bins = mel_frames.shape
    token_rows = cotangent.shape[1]
    model_width = stem_weight.shape[2]
    feed_width = hidden_weight.shape[1]
    head_count = HEADS
    head_size = model_width // head_count
    score_scale = head_size ** (-0.5)
    frame_index = lax.axis_index("frame")
    positions = sinusoid(frame_index * token_rows, token_rows, model_width)
    stem_matrix = stem_weight.reshape(3 * mel_bins, model_width)
    reduce_matrix = reduce_weight.reshape(3 * model_width, model_width)
    joint_weight = jnp.concatenate([query_weight, key_weight, value_weight], axis=1)
    joint_bias = jnp.concatenate([query_bias, jnp.zeros_like(query_bias), value_bias])
    live_count = window_count[0]

    def window_pass(slot_index, carry):
        totals, layer_output, mel_gradient = carry
        alive = (slot_index < live_count).astype(jnp.float32)
        mel_window = lax.dynamic_index_in_dim(mel_frames, slot_index, 0, keepdims=False)
        cotangent_window = lax.dynamic_index_in_dim(
            cotangent, slot_index, 0, keepdims=False
        ).astype(jnp.float32)
        extended = extended_2(mel_window, (("frame", 0),), 1)
        stem_columns = jnp.concatenate(
            [extended[0:frame_rows], extended[1 : frame_rows + 1], extended[2 : frame_rows + 2]],
            axis=1,
        )
        stem_linear = times_matrix(stem_columns, stem_matrix) + stem_bias
        stem_active = gelu_exact(stem_linear).astype(jnp.bfloat16)
        edge_row = from_behind(stem_active[frame_rows - 1 :], "frame", 1)
        joined_active = jnp.concatenate([edge_row, stem_active], axis=0)
        conv_columns = jnp.concatenate(
            [
                joined_active[0:frame_rows:2],
                joined_active[1:frame_rows:2],
                joined_active[2 : frame_rows + 1 : 2],
            ],
            axis=1,
        )
        conv_linear = times_matrix(conv_columns, reduce_matrix) + reduce_bias
        stream = gelu_exact(conv_linear) + positions
        first_normed = layer_norm(stream, first_gain, first_shift).astype(jnp.bfloat16)
        joint = (times_matrix(first_normed, joint_weight) + joint_bias).astype(jnp.bfloat16)
        query_flat = joint[:, :model_width]
        query_heads = query_flat.reshape(token_rows, head_count, head_size)
        keyval_local = joint[:, model_width:]
        keyval_whole = lax.all_gather(keyval_local, "frame", axis=0, tiled=True)
        window_tokens = keyval_whole.shape[0]
        key_heads = keyval_whole[:, :model_width].reshape(window_tokens, head_count, head_size)
        value_heads = keyval_whole[:, model_width:].reshape(window_tokens, head_count, head_size)
        scores = (
            jnp.einsum("qhd,khd->hqk", query_heads, key_heads, preferred_element_type=jnp.float32)
            * score_scale
        )
        row_max = jnp.max(scores, axis=-1, keepdims=True)
        exponent = jnp.exp(scores - row_max)
        row_sum = jnp.sum(exponent, axis=-1, keepdims=True)
        probs = exponent / row_sum
        attention_weights = probs.astype(jnp.bfloat16)
        attended = jnp.einsum(
            "hqk,khd->qhd", attention_weights, value_heads, preferred_element_type=jnp.float32
        )
        attended = attended.reshape(token_rows, model_width).astype(jnp.bfloat16)
        mixed = stream + times_matrix(attended, output_weight) + output_bias
        second_normed = layer_norm(mixed, second_gain, second_shift).astype(jnp.bfloat16)
        hidden_linear = times_matrix(second_normed, hidden_weight) + hidden_bias
        hidden_active = gelu_exact(hidden_linear).astype(jnp.bfloat16)
        output_rows = mixed + times_matrix(hidden_active, return_weight) + return_bias
        feed_grad = cotangent_window.astype(jnp.bfloat16)
        return_bias_grad = column_total(feed_grad)
        return_weight_grad = outer_total(hidden_active, feed_grad)
        hidden_grad = gelu_pull(hidden_linear, times_transpose(feed_grad, return_weight)).astype(
            jnp.bfloat16
        )
        hidden_bias_grad = column_total(hidden_grad)
        hidden_weight_grad = outer_total(second_normed, hidden_grad)
        mixed_inner, second_gain_grad, second_shift_grad = norm_pull(
            mixed, second_gain, second_shift, times_transpose(hidden_grad, hidden_weight)
        )
        mixed_grad = cotangent_window + mixed_inner
        branch_grad = mixed_grad.astype(jnp.bfloat16)
        output_bias_grad = column_total(branch_grad)
        output_weight_grad = outer_total(attended, branch_grad)
        attended_flat = times_transpose(branch_grad, output_weight).astype(jnp.bfloat16)
        attended_grad = attended_flat.reshape(token_rows, head_count, head_size)
        keyval_back = lax.all_gather(keyval_local, "frame", axis=0, tiled=True)
        key_back = keyval_back[:, :model_width].reshape(window_tokens, head_count, head_size)
        value_back = keyval_back[:, model_width:].reshape(window_tokens, head_count, head_size)
        weight_grad = jnp.einsum(
            "qhd,khd->hqk", attended_grad, value_back, preferred_element_type=jnp.float32
        )
        row_delta = jnp.sum(weight_grad * probs, axis=-1, keepdims=True)
        score_grad = (probs * (weight_grad - row_delta)).astype(jnp.bfloat16)
        query_grad = (
            jnp.einsum("hqk,khd->qhd", score_grad, key_back, preferred_element_type=jnp.float32)
            * score_scale
        )
        query_grad = query_grad.astype(jnp.bfloat16).reshape(token_rows, model_width)
        key_term = (
            jnp.einsum("hqk,qhd->khd", score_grad, query_heads, preferred_element_type=jnp.float32)
            * score_scale
        )
        value_term = jnp.einsum(
            "hqk,qhd->khd", attention_weights, attended_grad, preferred_element_type=jnp.float32
        )
        keyval_grad = lax.psum_scatter(
            jnp.concatenate(
                [
                    key_term.reshape(token_rows * lax.axis_size("frame"), model_width),
                    value_term.reshape(token_rows * lax.axis_size("frame"), model_width),
                ],
                axis=1,
            ),
            "frame",
            scatter_dimension=0,
            tiled=True,
        ).astype(jnp.bfloat16)
        joint_grad = jnp.concatenate([query_grad, keyval_grad], axis=1)
        joint_weight_grad = outer_total(first_normed, joint_grad)
        joint_bias_grad = column_total(joint_grad)
        stream_inner, first_gain_grad, first_shift_grad = norm_pull(
            stream, first_gain, first_shift, times_transpose(joint_grad, joint_weight)
        )
        stream_grad = mixed_grad + stream_inner
        conv_grad = gelu_pull(conv_linear, stream_grad).astype(jnp.bfloat16)
        reduce_bias_grad = column_total(conv_grad)
        reduce_matrix_grad = outer_total(conv_columns, conv_grad)
        columns_grad = times_transpose(conv_grad, reduce_matrix)
        pair_grad = columns_grad[:, : 2 * model_width].reshape(frame_rows, model_width)
        third_grad = columns_grad[:, 2 * model_width :]
        third_spread = jnp.stack([jnp.zeros_like(third_grad), third_grad], axis=1).reshape(
            frame_rows, model_width
        )
        incoming = from_behind(pair_grad[0:1], "frame", -1)
        active_grad = jnp.concatenate([pair_grad[1:], incoming], axis=0) + third_spread
        stem_grad = gelu_pull(stem_linear, active_grad).astype(jnp.bfloat16)
        stem_bias_grad = column_total(stem_grad)
        stem_matrix_grad = outer_total(stem_columns, stem_grad)
        mel_columns_grad = times_transpose(stem_grad, stem_matrix)
        extended_grad = (
            jnp.pad(mel_columns_grad[:, :mel_bins], ((0, 2), (0, 0)))
            + jnp.pad(mel_columns_grad[:, mel_bins : 2 * mel_bins], ((1, 1), (0, 0)))
            + jnp.pad(mel_columns_grad[:, 2 * mel_bins :], ((2, 0), (0, 0)))
        )
        rims = jnp.stack([extended_grad[0], extended_grad[frame_rows + 1]], axis=0)
        rim_rows = extended_2(rims, (("frame", 0),), 1)
        mel_rows = (
            extended_grad[1 : frame_rows + 1]
            + jnp.pad(rim_rows[0:1], ((0, frame_rows - 1), (0, 0)))
            + jnp.pad(rim_rows[3:4], ((frame_rows - 1, 0), (0, 0)))
        )
        gradients = (
            stem_matrix_grad,
            stem_bias_grad,
            reduce_matrix_grad,
            reduce_bias_grad,
            first_gain_grad,
            first_shift_grad,
            joint_weight_grad,
            joint_bias_grad,
            output_weight_grad,
            output_bias_grad,
            second_gain_grad,
            second_shift_grad,
            hidden_weight_grad,
            hidden_bias_grad,
            return_weight_grad,
            return_bias_grad,
        )
        totals = tuple((earlier + alive * fresh for earlier, fresh in zip(totals, gradients)))
        layer_output = lax.dynamic_update_index_in_dim(
            layer_output, (output_rows * alive).astype(jnp.bfloat16), slot_index, 0
        )
        mel_gradient = lax.dynamic_update_index_in_dim(
            mel_gradient, mel_rows * alive, slot_index, 0
        )
        return (totals, layer_output, mel_gradient)

    starting = (
        jnp.zeros((3 * mel_bins, model_width), jnp.float32),
        jnp.zeros((model_width,), jnp.float32),
        jnp.zeros((3 * model_width, model_width), jnp.float32),
        jnp.zeros((model_width,), jnp.float32),
        jnp.zeros((model_width,), jnp.float32),
        jnp.zeros((model_width,), jnp.float32),
        jnp.zeros((model_width, 3 * model_width), jnp.float32),
        jnp.zeros((3 * model_width,), jnp.float32),
        jnp.zeros((model_width, model_width), jnp.float32),
        jnp.zeros((model_width,), jnp.float32),
        jnp.zeros((model_width,), jnp.float32),
        jnp.zeros((model_width,), jnp.float32),
        jnp.zeros((model_width, feed_width), jnp.float32),
        jnp.zeros((feed_width,), jnp.float32),
        jnp.zeros((feed_width, model_width), jnp.float32),
        jnp.zeros((model_width,), jnp.float32),
    )
    empty_output = jnp.zeros((slot_total, token_rows, model_width), jnp.bfloat16)
    empty_gradient = jnp.zeros((slot_total, frame_rows, mel_bins), jnp.float32)
    totals, layer_output, mel_gradient = lax.fori_loop(
        0, slot_total, window_pass, (starting, empty_output, empty_gradient)
    )
    (
        stem_total,
        stem_bias_total,
        reduce_total,
        reduce_bias_total,
        first_gain_total,
        first_shift_total,
        joint_total,
        joint_bias_total,
        output_total,
        output_bias_total,
        second_gain_total,
        second_shift_total,
        hidden_total,
        hidden_bias_total,
        return_total,
        return_bias_total,
    ) = totals
    (
        stem_total,
        stem_bias_total,
        reduce_total,
        reduce_bias_total,
        first_gain_total,
        first_shift_total,
        joint_total,
        joint_bias_total,
        output_total,
        output_bias_total,
        second_gain_total,
        second_shift_total,
        hidden_total,
        hidden_bias_total,
        return_total,
        return_bias_total,
    ) = lax.psum(
        (
            stem_total,
            stem_bias_total,
            reduce_total,
            reduce_bias_total,
            first_gain_total,
            first_shift_total,
            joint_total,
            joint_bias_total,
            output_total,
            output_bias_total,
            second_gain_total,
            second_shift_total,
            hidden_total,
            hidden_bias_total,
            return_total,
            return_bias_total,
        ),
        ("dp", "frame"),
    )
    return (
        layer_output,
        mel_gradient,
        stem_total.reshape(3, mel_bins, model_width),
        stem_bias_total,
        reduce_total.reshape(3, model_width, model_width),
        reduce_bias_total,
        first_gain_total,
        first_shift_total,
        joint_total[:, :model_width],
        joint_bias_total[:model_width],
        joint_total[:, model_width : 2 * model_width],
        joint_total[:, 2 * model_width :],
        joint_bias_total[2 * model_width :],
        output_total,
        output_bias_total,
        second_gain_total,
        second_shift_total,
        hidden_total,
        hidden_bias_total,
        return_total,
        return_bias_total,
    )


def solution(mesh):
    return jax.shard_map(
        on_device,
        mesh=mesh,
        in_specs=(
            P("dp", "frame", None),
            P("dp"),
            P(),
            P(),
            P(),
            P(),
            P(),
            P(),
            P(),
            P(),
            P(),
            P(),
            P(),
            P(),
            P(),
            P(),
            P(),
            P(),
            P(),
            P(),
            P(),
            P("dp", "frame", None),
        ),
        out_specs=(
            P("dp", "frame", None),
            P("dp", "frame", None),
            P(),
            P(),
            P(),
            P(),
            P(),
            P(),
            P(),
            P(),
            P(),
            P(),
            P(),
            P(),
            P(),
            P(),
            P(),
            P(),
            P(),
            P(),
            P(),
        ),
        check_vma=False,
    )
```

profile of v0, /device:TPU:0, one launch (start us, length us, event | category | flops | bytes accessed | tf_op | source)
XLA Modules:
  0.0 806.8 jit_solution(12570393551199166072)
XLA Ops:
  12.3 487.0 %while.50 = (s32[]{:T(128)}, f32[240,512]{1,0:T(8,128)}, f32[512]{0:T(512)}, f32[1536,512]{1,0:T(8,128)}, f32[512]{0:T(512)}, /*index=5*/f32[512]{0:T(512)}, f32...) while((s32[]{:T(128)}, f32[240,512]{1,0:T(8,128)}, ...), condition=%wide.region_23.24_spmd.clone, body=%wide.region_0.23_spmd.clone.sunk | while | flops 13137714176 | bytes 643867520 | solution.py:306
  15.0 3.0 collective-permute-start.1
  18.8 5.1 multiply_convert_fusion.6
  24.0 4.4 collective-permute-start.2
  31.1 5.1 fusion.220
  39.4 30.5 %all-gather.2.cloned.1.call-done = bf16[1504,1024]{1,0:T(8,128)(2,1)} async-done(((bf16[376,1024]{1,0:T(8,128)(2,1)}), bf16[1504,1024]{1,0:T(8,128)(2,1)}) %all-gather.2.cloned.1.call-update) | async-done | bytes 3080208 | tf_op jit(solution)/shard_map/while/body/eval_jaxpr/all_gather | solution.py:154
  69.8 3.3 fusion.223
  76.4 10.8 %fusion.224 = (f32[8,376]{1,0:T(8,128)S(1)}, f32[8,376,1504]{2,1,0:T(8,128)}) fusion(bf16[376,8,64]{0,2,1:T(8,128)(2,1)} %bitcast.194, bf16[1504,8,64]{0,2,1:T(8,128)(2,1)S(1)} %bitcast.188), kind=kOutput, calls=%fused_computation.179.clone.1 | convolution fusion | flops 592649664 | bytes 20033280 | tf_op jit(solution)/shard_map/while/body/eval_jaxpr/sub | solution.py:163
  87.2 9.6 %fusion.225 = bf16[8,64,376]{2,1,0:T(8,128)(2,1)S(1)} fusion(bf16[1504,8,64]{0,2,1:T(8,128)(2,1)} %bitcast.197, f32[8,376,1504]{2,1,0:T(8,128)} %get-tuple-element.1619, f32[8,376]{1,0:T(8,128)S(1)} %get-tuple-element.1620), kind=kOutput, calls=%fused_computation.70.clone.1 | convolution fusion | flops 588316672 | bytes 20033280 | tf_op jit(solution)/shard_map/while/body/eval_jaxpr/hqk,khd->qhd/dot_general | solution.py:167
  98.5 8.3 %multiply_convert_fusion.7 = (bf16[376,2048]{1,0:T(8,128)(2,1)}, f32[376,2048]{1,0:T(8,128)S(1)}, f32[376,2048]{1,0:T(8,128)S(1)}) fusion(f32[2048]{0:T(1024)S(1)} %get-tuple-element.1779, bf16[512,2048]{1,0:T(8,128)(2,1)S(1)} %copy-done.73, f32[376,512]{1,0:T(8,128)S(1)} %get-tuple-element.1621, f32[512]{0:T(512)S(1)} %get-tuple-element.1777, ...), kind=kOutput, calls=%fused_computation.23.clone.1 | convolution fusion | flops 840314880 | bytes 10582976 | tf_op jit(solution)/shard_map/while/body/eval_jaxpr/dot_general | solution.py:57
  112.9 7.6 fusion.229
  120.6 11.7 %multiply_reduce_fusion.16 = (f32[8,376]{1,0:T(8,128)S(1)}, f32[8,376,1504]{2,1,0:T(8,128)}) fusion(f32[8,376,1504]{2,1,0:T(8,128)} %get-tuple-element.1619, f32[8,376]{1,0:T(8,128)S(1)} %get-tuple-element.1620, bf16[376,8,64]{0,2,1:T(8,128)(2,1)S(1)} %bitcast.202, bf16[1504,8,64]{0,2,1:T(8,128)(2,1)S(1)} %bitcast.198), kind=kOutput, calls=%fused_computation.2.clone.1 | convolution fusion | flops 592645184 | bytes 38141440 | tf_op jit(solution)/shard_map/while/body/eval_jaxpr/qhd,khd->hqk/dot_general | solution.py:196
  132.3 12.6 %multiply_convert_fusion.8 = bf16[8,376,1504]{2,1,0:T(8,128)(2,1)S(1)} fusion(f32[8,376,1504]{2,1,0:T(8,128)} %get-tuple-element.1631, f32[8,376]{1,0:T(8,128)S(1)} %get-tuple-element.1632, f32[8,376,1504]{2,1,0:T(8,128)} %get-tuple-element.1619, f32[8,376]{1,0:T(8,128)S(1)} %get-tuple-element.1620), kind=kLoop, calls=%fused_computation.1.clone.1 | loop fusion | flops 18096128 | bytes 45264384 | tf_op jit(solution)/shard_map/while/body/eval_jaxpr/convert_element_type | solution.py:200
  148.4 3.0 pad_maximum_fusion.20
  151.5 6.8 copy.82
  160.7 2.6 fusion.237
  164.2 3.8 select_add_fusion.29
  174.2 2.7 fusion.230
  177.0 39.4 %reduce-scatter.6.cloned.1.call-done = f32[376,1024]{1,0:T(8,128)} async-done(((f32[1504,1024]{1,0:T(8,128)}), f32[376,1024]{1,0:T(8,128)}) %reduce-scatter.6.cloned.1.call-update) | async-done | bytes 1540112 | tf_op jit(solution)/shard_map/while
  221.4 2.7 convert_reduce_fusion.13
  232.1 2.7 fusion.234
  241.9 2.6 convert_reduce_fusion.14
  247.7 3.7 collective-permute-start.5
  256.4 4.3 collective-permute-start.1
  261.5 5.1 multiply_convert_fusion.6
  266.6 4.0 collective-permute-start.2
  273.4 5.1 fusion.220
  281.7 30.1 %all-gather.2.cloned.1.call-done = bf16[1504,1024]{1,0:T(8,128)(2,1)} async-done(((bf16[376,1024]{1,0:T(8,128)(2,1)}), bf16[1504,1024]{1,0:T(8,128)(2,1)}) %all-gather.2.cloned.1.call-update) | async-done | bytes 3080208 | tf_op jit(solution)/shard_map/while/body/eval_jaxpr/all_gather | solution.py:154
  311.8 3.3 fusion.223
  318.4 10.4 %fusion.224 = (f32[8,376]{1,0:T(8,128)S(1)}, f32[8,376,1504]{2,1,0:T(8,128)}) fusion(bf16[376,8,64]{0,2,1:T(8,128)(2,1)} %bitcast.194, bf16[1504,8,64]{0,2,1:T(8,128)(2,1)S(1)} %bitcast.188), kind=kOutput, calls=%fused_computation.179.clone.1 | convolution fusion | flops 592649664 | bytes 20033280 | tf_op jit(solution)/shard_map/while/body/eval_jaxpr/sub | solution.py:163
  328.8 9.6 %fusion.225 = bf16[8,64,376]{2,1,0:T(8,128)(2,1)S(1)} fusion(bf16[1504,8,64]{0,2,1:T(8,128)(2,1)} %bitcast.197, f32[8,376,1504]{2,1,0:T(8,128)} %get-tuple-element.1619, f32[8,376]{1,0:T(8,128)S(1)} %get-tuple-element.1620), kind=kOutput, calls=%fused_computation.70.clone.1 | convolution fusion | flops 588316672 | bytes 20033280 | tf_op jit(solution)/shard_map/while/body/eval_jaxpr/hqk,khd->qhd/dot_general | solution.py:167
  340.1 8.3 %multiply_convert_fusion.7 = (bf16[376,2048]{1,0:T(8,128)(2,1)}, f32[376,2048]{1,0:T(8,128)S(1)}, f32[376,2048]{1,0:T(8,128)S(1)}) fusion(f32[2048]{0:T(1024)S(1)} %get-tuple-element.1779, bf16[512,2048]{1,0:T(8,128)(2,1)S(1)} %copy-done.73, f32[376,512]{1,0:T(8,128)S(1)} %get-tuple-element.1621, f32[512]{0:T(512)S(1)} %get-tuple-element.1777, ...), kind=kOutput, calls=%fused_computation.23.clone.1 | convolution fusion | flops 840314880 | bytes 10582976 | tf_op jit(solution)/shard_map/while/body/eval_jaxpr/dot_general | solution.py:57
  354.5 7.6 fusion.229
  362.2 11.7 %multiply_reduce_fusion.16 = (f32[8,376]{1,0:T(8,128)S(1)}, f32[8,376,1504]{2,1,0:T(8,128)}) fusion(f32[8,376,1504]{2,1,0:T(8,128)} %get-tuple-element.1619, f32[8,376]{1,0:T(8,128)S(1)} %get-tuple-element.1620, bf16[376,8,64]{0,2,1:T(8,128)(2,1)S(1)} %bitcast.202, bf16[1504,8,64]{0,2,1:T(8,128)(2,1)S(1)} %bitcast.198), kind=kOutput, calls=%fused_computation.2.clone.1 | convolution fusion | flops 592645184 | bytes 38141440 | tf_op jit(solution)/shard_map/while/body/eval_jaxpr/qhd,khd->hqk/dot_general | solution.py:196
  373.9 12.6 %multiply_convert_fusion.8 = bf16[8,376,1504]{2,1,0:T(8,128)(2,1)S(1)} fusion(f32[8,376,1504]{2,1,0:T(8,128)} %get-tuple-element.1631, f32[8,376]{1,0:T(8,128)S(1)} %get-tuple-element.1632, f32[8,376,1504]{2,1,0:T(8,128)} %get-tuple-element.1619, f32[8,376]{1,0:T(8,128)S(1)} %get-tuple-element.1620), kind=kLoop, calls=%fused_computation.1.clone.1 | loop fusion | flops 18096128 | bytes 45264384 | tf_op jit(solution)/shard_map/while/body/eval_jaxpr/convert_element_type | solution.py:200
  390.0 3.0 pad_maximum_fusion.20
  393.1 7.0 copy.82
  401.1 2.8 fusion.236
  403.8 2.7 fusion.237
  407.4 7.0 select_add_fusion.29
  418.7 2.7 fusion.230
  421.4 36.8 %reduce-scatter.6.cloned.1.call-done = f32[376,1024]{1,0:T(8,128)} async-done(((f32[1504,1024]{1,0:T(8,128)}), f32[376,1024]{1,0:T(8,128)}) %reduce-scatter.6.cloned.1.call-update) | async-done | bytes 1540112 | tf_op jit(solution)/shard_map/while
  463.3 2.6 convert_reduce_fusion.13
  473.8 4.7 fusion.234
  491.4 3.7 collective-permute-start.5
  500.1 45.0 %all-reduce.6 = (f32[512]{0:T(512)}, f32[512]{0:T(512)}, f32[512]{0:T(512)}, f32[512]{0:T(512)}, f32[1536]{0:T(1024)S(1)}, /*index=5*/f32[512]{0:T(512)}, f32[51...) all-reduce(f32[512]{0:T(512)S(1)} %copy-done.53, ...), channel_id=1, replica_groups=mesh['dp'=8,'frame'=4] {'dp','frame'}, use_global_device_ids=true, to_apply=%region_25.26 | all-reduce | flops 7680 | bytes 61440 | tf_op jit(solution)/shard_map/psum | solution.py:344
  545.6 239.5 %all-reduce.10.cloned.1.call-done = (f32[3,80,512]{2,1,0:T(8,128)}, f32[3,512,512]{2,1,0:T(8,128)}, f32[512,1536]{1,0:T(8,128)}, f32[512,512]{1,0:T(8,128)}, f32[512,2048]{1,0:T(8,128)}, /*index=5*/f32[2048,512]{1,0:T(8,128)}) async-done(((f32[3,80,512]{2,1,0:T(8,128)}, f32[3,512,512]{2,1,0:T(8,128)}, f32[512,1536]{1,0:T(8,128)}, f32[512,512]{1,0:T(8,128)}, f32[512,2048]{1,0:T(8,128)}, ...) | async-done | bytes 16220176 | tf_op jit(solution)/shard_map/psum | solution.py:344
  785.1 3.7 fusion.83
  (507 shorter events, 129.6 us)
Async XLA Ops:
  12.5 23.9 %copy-start.69 = (f32[1536]{0:T(1024)}, f32[1536]{0:T(1024)S(1)}, u32[]{:S(2)}) copy-start(f32[1536]{0:T(1024)S(1)} %get-tuple-element.1773) | copy-start | bytes 18436 | tf_op jit(solution)/shard_map/while
  12.6 57.3 %all-gather.2.cloned.1.call-start = ((), (), s32[]{:S(2)}) async-start(), calls=%async_computation.2 | async-start | bytes 3850240 | tf_op jit(solution)/shard_map/while/body/eval_jaxpr/all_gather | solution.py:154
  13.7 10.2 %copy-start.33 = (bf16[1,752,80]{2,1,0:T(8,128)(2,1)}, bf16[1,752,80]{2,1,0:T(8,128)(2,1)S(1)}, u32[]{:S(2)}) copy-start(bf16[1,752,80]{2,1,0:T(8,128)(2,1)S(1)} %copy.77) | copy-start | bytes 360964 | tf_op jit(solution)/shard_map/while
  13.7 4.3 collective-permute-start
  15.0 3.8 collective-permute-start.1
  24.0 6.1 collective-permute-start.2
  29.2 7.0 copy-start.25
  38.4 178.0 %reduce-scatter.6.cloned.1.call-start = ((), (), s32[]{:S(2)}) async-start(), calls=%async_computation.3 | async-start | bytes 7700480 | tf_op jit(solution)/shard_map/while
  76.4 10.8 %copy-start.4 = (bf16[1504,512]{0,1:T(8,128)(2,1)}, bf16[1504,512]{0,1:T(8,128)(2,1)S(1)}, u32[]{:S(2)}) copy-start(bf16[1504,512]{0,1:T(8,128)(2,1)S(1)} %copy.80) | copy-start | bytes 4620292 | tf_op jit(solution)/shard_map/while
  96.8 10.0 %copy-start.20 = (bf16[8,64,376]{2,1,0:T(8,128)(2,1)}, bf16[8,64,376]{2,1,0:T(8,128)(2,1)S(1)}, u32[]{:S(2)}) copy-start(bf16[8,64,376]{2,1,0:T(8,128)(2,1)S(1)} %fusion.225) | copy-start | bytes 1155076 | tf_op jit(solution)/shard_map/while
  98.5 8.3 %copy-start.15 = (bf16[2,376,512]{2,1,0:T(8,128)(2,1)S(1)}, bf16[2,376,512]{2,1,0:T(8,128)(2,1)}, u32[]{:S(2)}) copy-start(bf16[2,376,512]{2,1,0:T(8,128)(2,1)} %get-tuple-element.1768) | copy-start | bytes 2310148 | tf_op jit(solution)/shard_map/while
  98.5 8.3 %copy-start.74 = (bf16[2048,512]{1,0:T(8,128)(2,1)S(1)}, bf16[2048,512]{1,0:T(8,128)(2,1)}, u32[]{:S(2)}) copy-start(bf16[2048,512]{1,0:T(8,128)(2,1)} %get-tuple-element.1780) | copy-start | bytes 6291460 | tf_op jit(solution)/shard_map/while
  112.9 7.6 copy-start.19
  132.3 12.6 %copy-start.14 = (bf16[376,512]{0,1:T(8,128)(2,1)S(1)}, bf16[376,512]{0,1:T(8,128)(2,1)}, u32[]{:S(2)}) copy-start(bf16[376,512]{0,1:T(8,128)(2,1)} %copy.79) | copy-start | bytes 1155076 | tf_op jit(solution)/shard_map/while
  164.2 8.4 %slice-start = ((s8[9240576]{0:T(1024)(128)(4,1)}), s8[4194304]{0:T(1024)(128)(4,1)S(1)}, s32[]{:S(2)}) async-start(s8[9240576]{0:T(1024)(128)(4,1)} %bitcast.185), calls=%async_computation.4 | async-start | bytes 8388608 | tf_op jit(solution)/shard_map/while
  164.2 9.2 %slice-start.1 = ((s8[9240576]{0:T(1024)(128)(4,1)}), s8[4194304]{0:T(1024)(128)(4,1)S(1)}, s32[]{:S(2)}) async-start(s8[9240576]{0:T(1024)(128)(4,1)} %bitcast.185), calls=%async_computation.5 | async-start | bytes 8388608 | tf_op jit(solution)/shard_map/while
  235.1 6.8 collective-permute-start.3
  244.6 6.8 copy-start.34
  244.6 6.8 copy-start.43
  244.6 6.8 copy-start.86
  246.2 6.2 collective-permute-start.4
  247.7 4.8 collective-permute-start.5
  253.9 24.8 %copy-start.69 = (f32[1536]{0:T(1024)}, f32[1536]{0:T(1024)S(1)}, u32[]{:S(2)}) copy-start(f32[1536]{0:T(1024)S(1)} %get-tuple-element.1773) | copy-start | bytes 18436 | tf_op jit(solution)/shard_map/while
  254.0 57.9 %all-gather.2.cloned.1.call-start = ((), (), s32[]{:S(2)}) async-start(), calls=%async_computation.2 | async-start | bytes 3850240 | tf_op jit(solution)/shard_map/while/body/eval_jaxpr/all_gather | solution.py:154
  255.1 11.5 %copy-start.33 = (bf16[1,752,80]{2,1,0:T(8,128)(2,1)}, bf16[1,752,80]{2,1,0:T(8,128)(2,1)S(1)}, u32[]{:S(2)}) copy-start(bf16[1,752,80]{2,1,0:T(8,128)(2,1)S(1)} %copy.77) | copy-start | bytes 360964 | tf_op jit(solution)/shard_map/while
  255.1 5.6 collective-permute-start
  256.4 5.1 collective-permute-start.1
  266.6 5.8 collective-permute-start.2
  271.5 7.0 copy-start.25
  280.7 177.6 %reduce-scatter.6.cloned.1.call-start = ((), (), s32[]{:S(2)}) async-start(), calls=%async_computation.3 | async-start | bytes 7700480 | tf_op jit(solution)/shard_map/while
  318.4 10.4 %copy-start.4 = (bf16[1504,512]{0,1:T(8,128)(2,1)}, bf16[1504,512]{0,1:T(8,128)(2,1)S(1)}, u32[]{:S(2)}) copy-start(bf16[1504,512]{0,1:T(8,128)(2,1)S(1)} %copy.80) | copy-start | bytes 4620292 | tf_op jit(solution)/shard_map/while
  338.3 10.0 %copy-start.20 = (bf16[8,64,376]{2,1,0:T(8,128)(2,1)}, bf16[8,64,376]{2,1,0:T(8,128)(2,1)S(1)}, u32[]{:S(2)}) copy-start(bf16[8,64,376]{2,1,0:T(8,128)(2,1)S(1)} %fusion.225) | copy-start | bytes 1155076 | tf_op jit(solution)/shard_map/while
  340.1 8.3 %copy-start.15 = (bf16[2,376,512]{2,1,0:T(8,128)(2,1)S(1)}, bf16[2,376,512]{2,1,0:T(8,128)(2,1)}, u32[]{:S(2)}) copy-start(bf16[2,376,512]{2,1,0:T(8,128)(2,1)} %get-tuple-element.1768) | copy-start | bytes 2310148 | tf_op jit(solution)/shard_map/while
  340.1 8.3 %copy-start.74 = (bf16[2048,512]{1,0:T(8,128)(2,1)S(1)}, bf16[2048,512]{1,0:T(8,128)(2,1)}, u32[]{:S(2)}) copy-start(bf16[2048,512]{1,0:T(8,128)(2,1)} %get-tuple-element.1780) | copy-start | bytes 6291460 | tf_op jit(solution)/shard_map/while
  354.5 7.6 copy-start.19
  373.9 12.6 %copy-start.14 = (bf16[376,512]{0,1:T(8,128)(2,1)S(1)}, bf16[376,512]{0,1:T(8,128)(2,1)}, u32[]{:S(2)}) copy-start(bf16[376,512]{0,1:T(8,128)(2,1)} %copy.79) | copy-start | bytes 1155076 | tf_op jit(solution)/shard_map/while
  407.4 7.0 copy-start.6
  407.4 7.0 copy-start.23
  407.4 11.3 %slice-start = ((s8[9240576]{0:T(1024)(128)(4,1)}), s8[4194304]{0:T(1024)(128)(4,1)S(1)}, s32[]{:S(2)}) async-start(s8[9240576]{0:T(1024)(128)(4,1)} %bitcast.185), calls=%async_computation.4 | async-start | bytes 8388608 | tf_op jit(solution)/shard_map/while
  407.4 11.3 %slice-start.1 = ((s8[9240576]{0:T(1024)(128)(4,1)}), s8[4194304]{0:T(1024)(128)(4,1)S(1)}, s32[]{:S(2)}) async-start(s8[9240576]{0:T(1024)(128)(4,1)} %bitcast.185), calls=%async_computation.5 | async-start | bytes 8388608 | tf_op jit(solution)/shard_map/while
  478.9 6.8 collective-permute-start.3
  488.3 6.8 copy-start.34
  488.3 6.8 copy-start.43
  488.3 6.8 copy-start.86
  488.4 6.8 copy-start.88
  490.0 6.2 collective-permute-start.4
  491.4 4.8 collective-permute-start.5
  499.3 285.9 %all-reduce.10.cloned.1.call-start = ((), (), s32[]{:S(2)}) async-start(), calls=%async_computation.1 | async-start | bytes 32440320 | tf_op jit(solution)/shard_map/psum | solution.py:344
  (132 other events, 380.2 us)
Sparse Core Ops, SparseCore 0:
  38.5 31.3 all-gather.1
  158.4 57.9 reduce-scatter.5
  280.8 31.0 all-gather.1
  400.2 57.9 reduce-scatter.5
Sparse Core Ops, SparseCore 1:
  507.9 277.2 all-reduce.9
where the time goes:
time: 810 us; the launch traced here: 807 us
  waiting for transfers between devices  378 us (47%)
  matrix products  184 us (23%)
  local copies, waits for them, and re-layouts  95.3 us (12%)
  other arithmetic  50.6 us (6%)
  blocking collectives  45 us (6%)
  starting transfers between devices  31.6 us (4%)
  between operations  15.9 us (2%)
    psum x1, waiting for transfers between devices, on_device(): lax.psum((stem_total, stem_bias_total, reduce_total, reduce_bias_total, f...  240 us
    while x6, waiting for transfers between devices  76.2 us
    all_gather x2, waiting for transfers between devices, window_pass(): keyval_whole = lax.all_gather(keyval_local, 'frame', axis=0, tiled=True)  60.6 us
    psum x1, blocking collectives, on_device(): lax.psum((stem_total, stem_bias_total, reduce_total, reduce_bias_total, f...  45 us
    dot_general x12, matrix products, times_matrix(): return jnp.dot(left, right, preferred_element_type=jnp.float32)  44.9 us
    while x274, local copies, waits for them, and re-layouts  42.3 us
    dot_general x12, matrix products, outer_total(): lax.dot_general(left, right, (((0,), (0,)), ((), ())), preferred_element_...  32.8 us
    convert_element_type x2, other arithmetic, window_pass(): score_grad = (probs * (weight_grad - row_delta)).astype(jnp.bfloat16)  25.1 us
  transfers between devices with their start and end apart: 17, of which 7 were waited for; matrix products, arithmetic and copies ran while one was open for 6% of the time, Pallas kernels for 0%

commit v1 on v0

v1 whole, which is shorter than its diff:
```python
import math

import jax
import jax.numpy as jnp
from jax import lax
from jax.sharding import PartitionSpec as P

HEADS = 8
EPS = 1e-05
F32 = jnp.float32
BF16 = jnp.bfloat16
PHI_SLOPE = 0.28
PHI_POLY = (
    0.1167294156016242,
    0.06622785593379492,
    0.27197610469464767,
    -0.24067367858721922,
    0.3920693507793772,
    -0.10632905941542621,
)


def phi_parts(v):
    size = jnp.abs(v)
    t = 1.0 / (1.0 + PHI_SLOPE * size)
    bell = jnp.exp(-0.5 * v * v)
    poly = PHI_POLY[5]
    for c in PHI_POLY[4::-1]:
        poly = poly * t + c
    tail = poly * t * bell
    cdf = jnp.where(v >= 0, 1.0 - tail, tail)
    return cdf, bell * (1.0 / math.sqrt(2.0 * math.pi))


def gelu(v):
    cdf, _ = phi_parts(v)
    return v * cdf


def gelu_slope(v):
    cdf, pdf = phi_parts(v)
    return cdf + v * pdf


def dot(left, right):
    return jnp.dot(left, right, preferred_element_type=F32)


def dot_t(left, right):
    return lax.dot_general(left, right, (((1,), (1,)), ((), ())), preferred_element_type=F32)


def outer(left, right):
    return lax.dot_general(left, right, (((0,), (0,)), ((), ())), preferred_element_type=F32)


def column_total(x):
    return jnp.sum(x.astype(F32), axis=0)


def norm_parts(x):
    centred = x - jnp.mean(x, axis=-1, keepdims=True)
    r = lax.rsqrt(jnp.mean(centred * centred, axis=-1, keepdims=True) + EPS)
    return centred * r, r


def norm_pull(xhat, r, gain, dy):
    dh = dy * gain
    inner = r * (
        dh
        - jnp.mean(dh, axis=-1, keepdims=True)
        - xhat * jnp.mean(dh * xhat, axis=-1, keepdims=True)
    )
    return inner, column_total(dy * xhat), column_total(dy)


def positions_of(first, count, width):
    half = width // 2
    step = math.log(10000.0) / (half - 1)
    rate = jnp.exp(-step * jnp.arange(half, dtype=F32))[None, :]
    fine = math.gcd(count, 16)
    coarse = count // fine
    a = (first + fine * jnp.arange(coarse, dtype=jnp.int32)).astype(F32)[:, None] * rate
    b = jnp.arange(fine, dtype=jnp.int32).astype(F32)[:, None] * rate
    sa, ca = jnp.sin(a)[:, None, :], jnp.cos(a)[:, None, :]
    sb, cb = jnp.sin(b)[None, :, :], jnp.cos(b)[None, :, :]
    both = jnp.concatenate([sa * cb + ca * sb, ca * cb - sa * sb], axis=2)
    return both.reshape(count, width)


def on_device(
    mel_frames,
    window_count,
    stem_weight,
    stem_bias,
    reduce_weight,
    reduce_bias,
    first_gain,
    first_shift,
    query_weight,
    query_bias,
    key_weight,
    value_weight,
    value_bias,
    output_weight,
    output_bias,
    second_gain,
    second_shift,
    hidden_weight,
    hidden_bias,
    return_weight,
    return_bias,
    cotangent,
):
    S, piece_frames, mels = mel_frames.shape
    piece = cotangent.shape[1]
    D = stem_weight.shape[2]
    hd = D // HEADS
    scale = hd ** (-0.5)
    F = lax.axis_size("frame")
    G = F // S
    T = S * piece
    R = -(-(T + 2) // 128) * 128
    f = lax.axis_index("frame")
    s = f // G
    r = f % G
    alive = s < window_count[0]

    def gather_window(x):
        parts = []
        out = jnp.zeros((S * x.shape[1], x.shape[2]), x.dtype)
        for t in range(S):
            part = lax.dynamic_index_in_dim(x, (f + t) % S, 0, keepdims=False)
            perm = [(p, ((p % S + t) % S) * G + p // S) for p in range(F)]
            got = lax.ppermute(part, "frame", perm)
            j = (s - t) % S
            out = lax.dynamic_update_slice(out, got, (j * x.shape[1], 0))
        return out

    def scatter_window(x):
        n = x.shape[0] // S
        out = jnp.zeros((S, n, x.shape[1]), x.dtype)
        for t in range(S):
            j = (s - t) % S
            part = lax.dynamic_slice(x, (j * n, 0), (n, x.shape[1]))
            perm = [(((p % S + t) % S) * G + p // S, p) for p in range(F)]
            got = lax.ppermute(part, "frame", perm)
            out = lax.dynamic_update_slice(out, got[None], ((f + t) % S, 0, 0))
        return out

    down = [(i, i + 1) for i in range(F) if (i + 1) % G != 0]
    up = [(i + 1, i) for i in range(F) if (i + 1) % G != 0]

    def with_halo(x):
        before = lax.ppermute(x[T - 1 : T], "frame", down)
        after = lax.ppermute(x[0:1], "frame", up)
        gap = jnp.zeros((R - T - 2, x.shape[1]), x.dtype)
        return jnp.concatenate([x, after, gap, before], axis=0)

    mel = gather_window(mel_frames.reshape(S, piece, 2 * mels))
    cot = gather_window(cotangent)
    cot = jnp.where(alive, cot, jnp.zeros_like(cot))
    mel = with_halo(mel)
    odd_before = jnp.roll(mel[:, mels:], 1, axis=0)
    even_after = jnp.roll(mel[:, :mels], -1, axis=0)
    columns = jnp.concatenate([odd_before, mel, even_after], axis=1)
    stem_matrix = stem_weight.reshape(3 * mels, D)
    gap = jnp.zeros((mels, D), BF16)
    stem_pair = jnp.concatenate(
        [
            jnp.concatenate([stem_matrix, gap], axis=0),
            jnp.concatenate([gap, stem_matrix], axis=0),
        ],
        axis=1,
    )
    stem_bias2 = jnp.concatenate([stem_bias, stem_bias])
    stem_linear = dot(columns, stem_pair) + stem_bias2
    row = lax.broadcasted_iota(jnp.int32, (R, 1), 0)
    valid = (row < T) | ((row == T) & (r < G - 1)) | ((row == R - 1) & (r > 0))
    stem_active = jnp.where(valid, gelu(stem_linear), 0.0).astype(BF16)

    odd_active_before = jnp.roll(stem_active[:, D:], 1, axis=0)[:T]
    conv_columns = jnp.concatenate([odd_active_before, stem_active[:T]], axis=1)
    reduce_matrix = reduce_weight.reshape(3 * D, D)
    conv_linear = dot(conv_columns, reduce_matrix) + reduce_bias
    stream = gelu(conv_linear) + positions_of(r * T, T, D)
    xhat1, r1 = norm_parts(stream)
    first_normed = (xhat1 * first_gain + first_shift).astype(BF16)
    query = (dot(first_normed, query_weight) + query_bias).astype(BF16)
    key = dot(first_normed, key_weight).astype(BF16)
    value = (dot(first_normed, value_weight) + value_bias).astype(BF16)
    keyval = jnp.concatenate([key, value], axis=1)
    others = []
    for t in range(1, G):
        perm = [(i, (i // G) * G + (i % G + t) % G) for i in range(F)]
        others.append(lax.ppermute(keyval, "frame", perm))
    whole = jnp.concatenate([keyval] + others, axis=0)
    tokens = whole.shape[0]
    kh = whole[:, :D].reshape(tokens, HEADS, hd)
    vh = whole[:, D:].reshape(tokens, HEADS, hd)
    qh = query.reshape(T, HEADS, hd)
    scores = jnp.einsum("qhd,khd->hqk", qh, kh, preferred_element_type=F32) * scale
    exponent = jnp.exp(scores - jnp.max(scores, axis=-1, keepdims=True))
    probs = exponent / jnp.sum(exponent, axis=-1, keepdims=True)
    weights = probs.astype(BF16)
    attended = jnp.einsum("hqk,khd->qhd", weights, vh, preferred_element_type=F32)
    attended = attended.reshape(T, D).astype(BF16)
    mixed = stream + dot(attended, output_weight) + output_bias
    xhat2, r2 = norm_parts(mixed)
    second_normed = (xhat2 * second_gain + second_shift).astype(BF16)
    hidden_linear = dot(second_normed, hidden_weight) + hidden_bias
    hidden_cdf, hidden_pdf = phi_parts(hidden_linear)
    hidden_active = (hidden_linear * hidden_cdf).astype(BF16)
    layer = mixed + dot(hidden_active, return_weight) + return_bias
    layer = jnp.where(alive, layer, 0.0).astype(BF16)
    layer_output = scatter_window(layer)

    return_bias_grad = column_total(cot)
    return_weight_grad = outer(hidden_active, cot)
    slope = hidden_cdf + hidden_linear * hidden_pdf
    hidden_grad = (slope * dot_t(cot, return_weight)).astype(BF16)
    hidden_bias_grad = column_total(hidden_grad)
    hidden_weight_grad = outer(second_normed, hidden_grad)
    inner, second_gain_grad, second_shift_grad = norm_pull(
        xhat2, r2, second_gain, dot_t(hidden_grad, hidden_weight)
    )
    mixed_grad = cot.astype(F32) + inner
    branch_grad = mixed_grad.astype(BF16)
    output_bias_grad = column_total(branch_grad)
    output_weight_grad = outer(attended, branch_grad)

    early = lax.psum(
        (
            return_weight_grad.astype(BF16),
            hidden_weight_grad.astype(BF16),
            output_weight_grad.astype(BF16),
        ),
        ("dp", "frame"),
    )

    attended_grad = dot_t(branch_grad, output_weight).astype(BF16).reshape(T, HEADS, hd)
    weight_grad = jnp.einsum("qhd,khd->hqk", attended_grad, vh, preferred_element_type=F32)
    delta = jnp.sum(weight_grad * probs, axis=-1, keepdims=True)
    score_grad = (probs * (weight_grad - delta)).astype(BF16)
    query_grad = jnp.einsum("hqk,khd->qhd", score_grad, kh, preferred_element_type=F32) * scale
    query_grad = query_grad.astype(BF16).reshape(T, D)
    key_term = jnp.einsum("hqk,qhd->khd", score_grad, qh, preferred_element_type=F32) * scale
    value_term = jnp.einsum("hqk,qhd->khd", weights, attended_grad, preferred_element_type=F32)
    terms = jnp.concatenate([key_term.reshape(tokens, D), value_term.reshape(tokens, D)], axis=1)
    total = terms[:T]
    for t in range(1, G):
        perm = [((i // G) * G + (i % G + t) % G, i) for i in range(F)]
        back = lax.ppermute(terms[t * T : (t + 1) * T], "frame", perm)
        total = total + back
    key_grad = total[:, :D].astype(BF16)
    value_grad = total[:, D:].astype(BF16)
    query_weight_grad = outer(first_normed, query_grad)
    key_weight_grad = outer(first_normed, key_grad)
    value_weight_grad = outer(first_normed, value_grad)
    query_bias_grad = column_total(query_grad)
    value_bias_grad = column_total(value_grad)
    normed_grad = (
        dot_t(query_grad, query_weight)
        + dot_t(key_grad, key_weight)
        + dot_t(value_grad, value_weight)
    )
    inner, first_gain_grad, first_shift_grad = norm_pull(xhat1, r1, first_gain, normed_grad)
    stream_grad = mixed_grad + inner
    conv_grad = (gelu_slope(conv_linear) * stream_grad).astype(BF16)
    reduce_bias_grad = column_total(conv_grad)
    reduce_matrix_grad = outer(conv_columns, conv_grad)
    conv_ext = with_halo(conv_grad)
    conv_after = jnp.roll(conv_ext, -1, axis=0)
    pair_grad = dot_t(conv_ext, reduce_matrix[D:])
    third_grad = dot_t(conv_after, reduce_matrix[:D])
    active_grad = pair_grad + jnp.concatenate([jnp.zeros_like(third_grad), third_grad], axis=1)
    stem_grad = jnp.where(valid, gelu_slope(stem_linear) * active_grad, 0.0).astype(BF16)
    own = stem_grad[:T]
    totals = column_total(own)
    stem_bias_grad = totals[:D] + totals[D:]
    pair_matrix_grad = outer(columns[:T], own)
    stem_matrix_grad = pair_matrix_grad[: 3 * mels, :D] + pair_matrix_grad[mels:, D:]
    mel_columns = dot_t(stem_grad, stem_pair)
    mel_pair = (
        mel_columns[:, mels : 3 * mels]
        + jnp.concatenate(
            [
                jnp.roll(mel_columns[:, 3 * mels :], 1, axis=0),
                jnp.roll(mel_columns[:, :mels], -1, axis=0),
            ],
            axis=1,
        )
    )[:T]
    mel_gradient = scatter_window(mel_pair).reshape(S, piece_frames, mels)

    late = lax.psum(
        (
            reduce_matrix_grad.astype(BF16),
            query_weight_grad.astype(BF16),
            key_weight_grad.astype(BF16),
            value_weight_grad.astype(BF16),
            stem_matrix_grad.astype(BF16),
        ),
        ("dp", "frame"),
    )
    small = [
        stem_bias_grad,
        reduce_bias_grad,
        first_gain_grad,
        first_shift_grad,
        query_bias_grad,
        value_bias_grad,
        output_bias_grad,
        second_gain_grad,
        second_shift_grad,
        hidden_bias_grad,
        return_bias_grad,
    ]
    sizes = [v.shape[0] for v in small]
    packed = lax.psum(jnp.concatenate(small).reshape(-1, 128), ("dp", "frame")).reshape(-1)
    small = []
    at = 0
    for n in sizes:
        small.append(packed[at : at + n])
        at += n
    return_w, hidden_w, output_w = [x.astype(F32) for x in early]
    reduce_w, query_w, key_w, value_w, stem_w = [x.astype(F32) for x in late]
    return (
        layer_output,
        mel_gradient,
        stem_w.reshape(3, mels, D),
        small[0],
        reduce_w.reshape(3, D, D),
        small[1],
        small[2],
        small[3],
        query_w,
        small[4],
        key_w,
        value_w,
        small[5],
        output_w,
        small[6],
        small[7],
        small[8],
        hidden_w,
        small[9],
        return_w,
        small[10],
    )


def solution(mesh):
    cut = P("dp", "frame", None)
    return jax.shard_map(
        on_device,
        mesh=mesh,
        in_specs=(cut, P("dp")) + (P(),) * 19 + (cut,),
        out_specs=(cut, cut) + (P(),) * 19,
        check_vma=False,
    )
```

time: 810 us -> 483 us (0.60)
  waiting for transfers between devices: 378 us -> 120 us
  local copies, waits for them, and re-layouts: 95.3 us -> 40 us
  matrix products: 184 us -> 162 us
    psum x1, waiting for transfers between devices: 240 us -> 115 us  [on_device(): lax.psum((reduce_matrix_grad.astype(BF16), query_weight_grad.astype(BF16)...]
    while x6 -> x0, waiting for transfers between devices: 76.2 us -> none
    all_gather x2 -> x0, waiting for transfers between devices: 60.6 us -> none  [window_pass(): keyval_whole = lax.all_gather(keyval_local, 'frame', axis=0, tiled=True)]
    while x274 -> x0, local copies, waits for them, and re-layouts: 42.3 us -> none
    dot_general x46 -> x30, matrix products: 163 us -> 144 us  [the longest x1 27.8 us: on_device(): jnp.einsum('qhd,khd->hqk', attended_grad, vh, preferred_element_type=F32)]
    convert_element_type x3 -> x11, other arithmetic: 25.1 us -> 42.5 us  [the longest x1 30.1 us: on_device(): score_grad = (probs * (weight_grad - delta)).astype(BF16)]
    slice x34 -> x17, local copies, waits for them, and re-layouts: 26.8 us -> 10.1 us  [the longest x2 4.54 us: on_device(): kh = whole[:, :D].reshape(tokens, HEADS, hd)]
    reduce_sum x16 -> x6, other arithmetic: 14.1 us -> 4.56 us  [the longest x4 3.91 us: column_total(): return jnp.sum(x.astype(F32), axis=0)]
  transfers between devices with their start and end apart: 17 -> 15, of which waited for: 7 -> 4; matrix products, arithmetic and copies ran while one was open for 6% -> 13% of each run, Pallas kernels for 0% -> 0%
where the time goes in v1:
time: 483 us; the launch traced here: 475 us
  matrix products  162 us (34%)
  waiting for transfers between devices  120 us (25%)
  other arithmetic  58.1 us (12%)
  blocking collectives  52.9 us (11%)
  local copies, waits for them, and re-layouts  40 us (8%)
  starting transfers between devices  26.7 us (6%)
  between operations  16.4 us (3%)
    psum x1, waiting for transfers between devices, on_device(): lax.psum((reduce_matrix_grad.astype(BF16), query_weight_grad.astype(BF16)...  115 us
    psum x1, blocking collectives, on_device(): lax.psum(jnp.concatenate(small).reshape(-1, 128), ('dp', 'frame'))  52.9 us
    convert_element_type x1, other arithmetic, on_device(): score_grad = (probs * (weight_grad - delta)).astype(BF16)  30.1 us
    dot_general x1, matrix products, on_device(): jnp.einsum('qhd,khd->hqk', attended_grad, vh, preferred_element_type=F32)  27.8 us
    dot_general x8, matrix products, dot(): return jnp.dot(left, right, preferred_element_type=F32)  24.7 us
    dot_general x9, matrix products, dot_t(): lax.dot_general(left, right, (((1,), (1,)), ((), ())), preferred_element_...  23.1 us
    sub x1, matrix products, on_device(): exponent = jnp.exp(scores - jnp.max(scores, axis=-1, keepdims=True))  18.2 us
    dot_general x8, matrix products, outer(): lax.dot_general(left, right, (((0,), (0,)), ((), ())), preferred_element_...  16.2 us
  transfers between devices with their start and end apart: 15, of which 4 were waited for; matrix products, arithmetic and copies ran while one was open for 13% of the time, Pallas kernels for 0%

profile of v1, /device:TPU:0, one launch (start us, length us, event | category | flops | bytes accessed | tf_op | source)
XLA Modules:
  0.0 475.4 jit_solution(15146913704868188641)
XLA Ops:
  10.2 3.6 collective-permute-start.1
  16.4 2.0 collective-permute-done.1
  18.4 2.8 collective-permute-start.2
  22.6 1.6 collective-permute-done.3
  24.2 6.2 %select_convert_fusion.1 = (bf16[768,1024]{1,0:T(8,128)(2,1)S(1)}, f32[768,1024]{1,0:T(8,128)}) fusion(f32[1024]{0:T(1024)S(1)} %pad_maximum_fusion.15, pred[768]{0:T(1024)(128)(4,1)S(1)} %fusion.90, bf16[240,512]{1,0:T(8,128)(2,1)} %bitcast.143, bf16[1,160]{1,0:T(2,128)(2,1)S(1)} %collective-permute-done.2, bf16[14,160]{1,0:T(8,128)(2,1)S(1)} %broadcast_in_dim.36, ...), kind=kOutput, calls=%fused_computation.30 | convolution fusion | flops 531988480 | bytes 5215296 | tf_op jit(solution)/shard_map/dot_general | solution.py:46
  33.0 3.9 fusion.125
  42.9 4.7 collective-permute-start.7
  50.0 1.4 add_convert_fusion.1
  57.2 1.7 pad_maximum_fusion.1
  59.0 1.9 fusion.126
  60.9 2.6 copy.62
  63.5 2.6 copy.60
  66.1 18.2 %fusion.131 = (f32[8,752]{1,0:T(8,128)S(1)}, f32[8,752,1504]{2,1,0:T(8,128)}) fusion(bf16[752,8,64]{0,2,1:T(8,128)(2,1)S(1)} %bitcast.123, bf16[1504,8,64]{0,2,1:T(8,128)(2,1)} %bitcast.117), kind=kOutput, calls=%fused_computation.248 | convolution fusion | flops 1185297920 | bytes 38526464 | tf_op jit(solution)/shard_map/sub | solution.py:203
  84.3 15.6 %fusion.18 = bf16[8,64,752]{2,1,0:T(8,128)(2,1)} fusion(bf16[1504,8,64]{0,2,1:T(8,128)(2,1)} %bitcast.130, f32[8,752]{1,0:T(8,128)S(1)} %get-tuple-element.123, bf16[752,8,64]{0,2,1:T(8,128)(2,1)S(1)} %bitcast.124, bf16[1504,8,64]{0,2,1:T(8,128)(2,1)} %bitcast.118), kind=kOutput, calls=%fused_computation.78 | convolution fusion | flops 2352889344 | bytes 4644352 | tf_op jit(solution)/shard_map/hqk,khd->qhd/dot_general | solution.py:206
  99.9 2.3 fusion.132
  102.6 8.0 %multiply_convert_fusion.2 = (bf16[752,2048]{1,0:T(8,128)(2,1)}, f32[752,2048]{1,0:T(8,128)S(1)}) fusion(f32[2048]{0:T(1024)S(1)} %copy-done.87, bf16[512,2048]{1,0:T(8,128)(2,1)S(1)} %copy-done, f32[752,512]{1,0:T(8,128)S(1)} %get-tuple-element.126, f32[512]{0:T(512)S(1)} %copy-done.63, f32[512]{0:T(512)S(1)} %copy-done.61, f32[752]{0:T(1024)S(1)} %add_rsqrt_fusion, ...), kind=kOutput, calls=%fused_computation.20 | convolution fusion | flops 1615945728 | bytes 12896128 | tf_op jit(solution)/shard_map/dot_general | solution.py:46
  110.7 7.6 %convert_reduce_fusion = (f32[2048]{0:T(1024)}, bf16[752,2048]{1,0:T(8,128)(2,1)S(1)}) fusion(bf16[2048,512]{1,0:T(8,128)(2,1)S(1)} %copy-done.84, bf16[752,512]{1,0:T(8,128)(2,1)S(1)} %copy-done.19, pred[]{:T(512)S(6)} %lt.84, f32[752,2048]{1,0:T(8,128)S(1)} %get-tuple-element.128, f32[2048]{0:T(1024)S(1)} %copy-done.87), kind=kOutput, calls=%fused_computation.18 | convolution fusion | flops 1622104064 | bytes 12124161 | tf_op jit(solution)/shard_map/dot_general | solution.py:50
  118.3 2.7 multiply_reduce_fusion.2
  121.1 1.4 convert_reduce_fusion.4
  122.5 1.5 convolution_convert_fusion.3
  124.0 2.3 copy.63
  126.3 15.0 %fusion.5 = f32[8,64,1504]{2,1,0:T(8,128)} fusion(bf16[752,8,64]{0,2,1:T(8,128)(2,1)} %bitcast.135, f32[8,752]{1,0:T(8,128)S(1)} %get-tuple-element.123, bf16[752,8,64]{0,2,1:T(8,128)(2,1)S(1)} %bitcast.125, bf16[1504,8,64]{0,2,1:T(8,128)(2,1)} %bitcast.119), kind=kOutput, calls=%fused_computation.10 | convolution fusion | flops 2352504320 | bytes 6184448 | tf_op jit(solution)/shard_map/hqk,qhd->khd/dot_general | solution.py:248
  141.2 27.8 %multiply_reduce_fusion = (f32[8,752]{1,0:T(8,128)S(1)}, f32[8,752,1504]{2,1,0:T(8,128)}) fusion(f32[8,752,1504]{2,1,0:T(8,128)} %get-tuple-element.124, f32[8,752]{1,0:T(8,128)S(1)} %get-tuple-element.123, bf16[752,8,64]{0,2,1:T(8,128)(2,1)} %bitcast.136, bf16[1504,8,64]{0,2,1:T(8,128)(2,1)} %bitcast.131), kind=kOutput, calls=%fused_computation.2 | convolution fusion | flops 1185290368 | bytes 74742784 | tf_op jit(solution)/shard_map/qhd,khd->hqk/dot_general | solution.py:242
  169.1 30.1 %multiply_convert_fusion = bf16[8,752,1504]{2,1,0:T(8,128)(2,1)} fusion(f32[8,752,1504]{2,1,0:T(8,128)} %get-tuple-element.131, f32[8,752]{1,0:T(8,128)S(1)} %get-tuple-element.130, f32[8,752,1504]{2,1,0:T(8,128)} %get-tuple-element.124, f32[8,752]{1,0:T(8,128)S(1)} %get-tuple-element.123), kind=kLoop, calls=%fused_computation.1 | loop fusion | flops 36192256 | bytes 90528768 | tf_op jit(solution)/shard_map/convert_element_type | solution.py:244
  199.2 11.2 %convolution_multiply_fusion = f32[8,64,1504]{2,1,0:T(8,128)} fusion(bf16[752,8,64]{0,2,1:T(8,128)(2,1)S(1)} %bitcast.126, bf16[8,752,1504]{2,1,0:T(8,128)(2,1)} %multiply_convert_fusion), kind=kOutput, calls=%fused_computation.27 | convolution fusion | flops 1158922240 | bytes 21946368 | tf_op jit(solution)/shard_map/hqk,qhd->khd/dot_general | solution.py:247
  210.4 3.6 copy.64
  214.0 3.5 copy.65
  217.5 2.3 pad_maximum_fusion
  221.5 1.8 select_convert_fusion.2
  223.3 1.4 collective-permute-start.5
  224.7 3.1 collective-permute-start.6
  227.8 10.0 %convert_reduce_fusion.3 = (f32[8,64]{1,0:T(8,128)S(1)}, bf16[8,64,752]{2,1,0:T(8,128)(2,1)S(1)}) fusion(bf16[1504,8,64]{0,2,1:T(8,128)(2,1)S(1)} %bitcast.120, bf16[8,752,1504]{2,1,0:T(8,128)(2,1)} %multiply_convert_fusion), kind=kOutput, calls=%fused_computation.50 | convolution fusion | flops 1159691776 | bytes 20408320 | tf_op jit(solution)/shard_map/hqk,khd->qhd/dot_general | solution.py:245
  241.8 3.2 convolution_convert_fusion
  245.0 3.4 convolution_convert_fusion.1
  253.4 2.0 convert_reduce_fusion.6
  255.5 2.6 convolution_convert_fusion.2
  258.1 1.4 convolution_convert_fusion.6
  261.0 3.2 collective-permute-start.11
  264.2 1.4 convolution_convert_fusion.7
  266.1 1.8 fusion.27
  268.3 4.7 select_convert_fusion
  277.8 2.2 fusion.86
  281.5 1.5 collective-permute-start.13
  283.5 52.9 %psum.64 = f32[56,128]{1,0:T(8,128)S(1)} all-reduce(f32[56,128]{1,0:T(8,128)S(1)} %bitcast.142), channel_id=1, replica_groups=mesh['dp'=8,'frame'=4] {'dp','frame'}, use_global_device_ids=true, to_apply=%region_23.24 | all-reduce | flops 7168 | bytes 57344 | tf_op jit(solution)/shard_map/psum | solution.py:320
  339.4 114.7 %all-reduce.6.cloned.1.call-done = (bf16[3,80,512]{2,1,0:T(8,128)(2,1)}, bf16[3,512,512]{2,1,0:T(8,128)(2,1)}, bf16[512,512]{1,0:T(8,128)(2,1)}, bf16[512,512]{1...) async-done(((bf16[3,80,512]{2,1,0:T(8,128)(2,1)}, ...) | async-done | bytes 8110096 | tf_op jit(solution)/shard_map/psum | solution.py:296
  454.1 4.3 convert_element_type.189
  458.4 2.6 convert_element_type.191
  461.0 2.1 reshape.331
  (318 shorter events, 50.4 us)
Async XLA Ops:
  7.2 95.4 %copy-start = (bf16[512,2048]{1,0:T(8,128)(2,1)S(1)}, bf16[512,2048]{1,0:T(8,128)(2,1)}, u32[]{:S(2)}) copy-start(bf16[512,2048]{1,0:T(8,128)(2,1)} %param.39) | copy-start | bytes 6291460
  7.2 446.9 %all-reduce.6.cloned.1.call-start = ((), (), s32[]{:S(2)}) async-start(), calls=%async_computation | async-start | bytes 16220160 | tf_op jit(solution)/shard_map/psum | solution.py:296
  8.6 6.7 %copy-start.77 = (f32[512]{0:T(512)S(1)}, f32[512]{0:T(512)}, u32[]{:S(2)}) copy-start(f32[512]{0:T(512)} %param.25) | copy-start | bytes 6148
  8.9 6.5 %collective-permute-start = (bf16[376,160]{1,0:T(8,128)(2,1)S(1)}, bf16[376,160]{1,0:T(8,128)(2,1)}, u32[]{:S(2)}, u32[]{:S(2)}) collective-permute-start(bf16[376,160]{1,0:T(8,128)(2,1)S(1)} %get-tuple-element.103), channel_id=1, source_target_pairs={{0,0},{1,2},{2,1},{3,3},{4,4},{5,6},{6,5},{7,7},{8,8},{9,10},{10,9... | collective-permute-start | bytes 360968 | tf_op jit(solution)/shard_map/ppermute | solution.py:135
  10.2 8.2 %collective-permute-start.1 = (bf16[376,160]{1,0:T(8,128)(2,1)S(1)}, bf16[376,160]{1,0:T(8,128)(2,1)S(1)}, u32[]{:S(2)}, u32[]{:S(2)}) collective-permute-start(bf16[376,160]{1,0:T(8,128)(2,1)S(1)} %get-tuple-element.102), channel_id=1, source_target_pairs={{0,2},{1,0},{2,3},{3,1},{4,6},{5,4},{6,7},{7,5},{8,10},{9,8},{10,1... | collective-permute-start | bytes 360968 | tf_op jit(solution)/shard_map/ppermute | solution.py:135
  15.3 15.1 %copy-start.73 = (f32[1024]{0:T(1024)}, f32[1024]{0:T(1024)S(1)}, u32[]{:S(2)}) copy-start(f32[1024]{0:T(1024)S(1)} %pad_maximum_fusion.15) | copy-start | bytes 12292
  18.4 12.0 %copy-start.50 = (bf16[752,160]{1,0:T(8,128)(2,1)}, bf16[752,160]{1,0:T(8,128)(2,1)S(1)}, u32[]{:S(2)}) copy-start(bf16[752,160]{1,0:T(8,128)(2,1)S(1)} %constant_dynamic-update-slice_fusion.14) | copy-start | bytes 721924
  18.4 4.1 collective-permute-start.2
  21.2 3.1 collective-permute-start.3
  22.5 7.9 %copy-start.82 = (pred[768]{0:T(1024)(128)(4,1)}, pred[768]{0:T(1024)(128)(4,1)S(1)}, u32[]{:S(2)}) copy-start(pred[768]{0:T(1024)(128)(4,1)S(1)} %fusion.90) | copy-start | bytes 2308
  22.5 7.9 %copy-start.96 = (bf16[1,80]{1,0:T(2,128)(2,1)}, bf16[1,80]{1,0:T(2,128)(2,1)S(1)}, u32[]{:S(2)}) copy-start(bf16[1,80]{1,0:T(2,128)(2,1)S(1)} %slice.265) | copy-start | bytes 484
  22.5 7.9 %copy-start.92 = (bf16[1,160]{1,0:T(2,128)(2,1)}, bf16[1,160]{1,0:T(2,128)(2,1)S(1)}, u32[]{:S(2)}) copy-start(bf16[1,160]{1,0:T(2,128)(2,1)S(1)} %collective-permute-done.2) | copy-start | bytes 964
  22.6 7.8 %copy-start.98 = (bf16[1,80]{1,0:T(2,128)(2,1)}, bf16[1,80]{1,0:T(2,128)(2,1)S(1)}, u32[]{:S(2)}) copy-start(bf16[1,80]{1,0:T(2,128)(2,1)S(1)} %slice.263) | copy-start | bytes 484
  24.2 6.2 %copy-start.94 = (bf16[1,160]{1,0:T(2,128)(2,1)}, bf16[1,160]{1,0:T(2,128)(2,1)S(1)}, u32[]{:S(2)}) copy-start(bf16[1,160]{1,0:T(2,128)(2,1)S(1)} %collective-permute-done.3) | copy-start | bytes 964
  24.2 6.2 %copy-start.71 = (bf16[14,160]{1,0:T(8,128)(2,1)}, bf16[14,160]{1,0:T(8,128)(2,1)S(1)}, u32[]{:S(2)}) copy-start(bf16[14,160]{1,0:T(8,128)(2,1)S(1)} %broadcast_in_dim.36) | copy-start | bytes 13444
  30.6 6.2 %copy-start.27 = (bf16[752,1024]{1,0:T(8,128)(2,1)}, bf16[752,1024]{1,0:T(8,128)(2,1)S(1)}, u32[]{:S(2)}) copy-start(bf16[752,1024]{1,0:T(8,128)(2,1)S(1)} %slice.268) | copy-start | bytes 4620292
  30.7 6.1 %copy-start.32 = (bf16[767,512]{1,0:T(8,128)(2,1)}, bf16[767,512]{1,0:T(8,128)(2,1)S(1)}, u32[]{:S(2)}) copy-start(bf16[767,512]{1,0:T(8,128)(2,1)S(1)} %slice.267) | copy-start | bytes 2356228
  30.8 6.1 %copy-start.80 = (bf16[1,512]{1,0:T(2,128)(2,1)}, bf16[1,512]{1,0:T(2,128)(2,1)S(1)}, u32[]{:S(2)}) copy-start(bf16[1,512]{1,0:T(2,128)(2,1)S(1)} %slice.266) | copy-start | bytes 3076
  38.3 11.6 %copy-start.34 = (bf16[752,512]{1,0:T(8,128)(2,1)}, bf16[752,512]{1,0:T(8,128)(2,1)S(1)}, u32[]{:S(2)}) copy-start(bf16[752,512]{1,0:T(8,128)(2,1)S(1)} %add_convert_fusion.3) | copy-start | bytes 2310148
  41.6 8.4 %copy-start.46 = (bf16[512,512]{1,0:T(8,128)(2,1)S(1)}, bf16[512,512]{1,0:T(8,128)(2,1)}, u32[]{:S(2)}) copy-start(bf16[512,512]{1,0:T(8,128)(2,1)} %param.30) | copy-start | bytes 1572868
  41.6 8.4 %copy-start.90 = (f32[512]{0:T(512)S(1)}, f32[512]{0:T(512)}, u32[]{:S(2)}) copy-start(f32[512]{0:T(512)} %param.31) | copy-start | bytes 6148
  41.6 15.6 %collective-permute-start.4 = (bf16[752,1024]{1,0:T(8,128)(2,1)}, bf16[752,1024]{1,0:T(8,128)(2,1)}, u32[]{:S(2)}, u32[]{:S(2)}) collective-permute-start(bf16[752,1024]{1,0:T(8,128)(2,1)} %pad_maximum_fusion.3), channel_id=1, source_target_pairs={{0,1},{1,0},{2,3},{3,2},{4,5},{5,4},{6,7},{7,6},{8,9},{9,8},{10,11... | collective-permute-start | bytes 4620296 | tf_op jit(solution)/shard_map/ppermute | solution.py:196
  42.9 10.0 %collective-permute-start.7 = (bf16[376,512]{1,0:T(8,128)(2,1)}, bf16[376,512]{1,0:T(8,128)(2,1)}, u32[]{:S(2)}, u32[]{:S(2)}) collective-permute-start(bf16[376,512]{1,0:T(8,128)(2,1)} %get-tuple-element.95), channel_id=1, source_target_pairs={{0,0},{1,2},{2,1},{3,3},{4,4},{5,6},{6,5},{7,7},{8,8},{9,10},{10,9... | collective-permute-start | bytes 1155080 | tf_op jit(solution)/shard_map/ppermute | solution.py:135
  47.6 7.7 %collective-permute-start.8 = (bf16[376,512]{1,0:T(8,128)(2,1)}, bf16[376,512]{1,0:T(8,128)(2,1)}, u32[]{:S(2)}, u32[]{:S(2)}) collective-permute-start(bf16[376,512]{1,0:T(8,128)(2,1)} %get-tuple-element.94), channel_id=1, source_target_pairs={{0,2},{1,0},{2,3},{3,1},{4,6},{5,4},{6,7},{7,5},{8,10},{9,8},{10,1... | collective-permute-start | bytes 1155080 | tf_op jit(solution)/shard_map/ppermute | solution.py:135
  84.3 15.6 %copy-start.24 = (bf16[512,512]{1,0:T(8,128)(2,1)S(1)}, bf16[512,512]{1,0:T(8,128)(2,1)}, u32[]{:S(2)}) copy-start(bf16[512,512]{1,0:T(8,128)(2,1)} %param.35) | copy-start | bytes 1572868
  84.3 15.6 %copy-start.76 = (f32[512]{0:T(512)S(1)}, f32[512]{0:T(512)}, u32[]{:S(2)}) copy-start(f32[512]{0:T(512)} %param.36) | copy-start | bytes 6148
  102.2 18.8 %copy-start.8 = (f32[752,512]{1,0:T(8,128)}, f32[752,512]{1,0:T(8,128)S(1)}, u32[]{:S(2)}) copy-start(f32[752,512]{1,0:T(8,128)S(1)} %get-tuple-element.126) | copy-start | bytes 4620292
  102.2 18.8 %copy-start.53 = (f32[752]{0:T(1024)}, f32[752]{0:T(1024)S(1)}, u32[]{:S(2)}) copy-start(f32[752]{0:T(1024)S(1)} %broadcast_multiply_fusion.4) | copy-start | bytes 9028
  102.6 18.4 %copy-start.55 = (f32[752]{0:T(1024)}, f32[752]{0:T(1024)S(1)}, u32[]{:S(2)}) copy-start(f32[752]{0:T(1024)S(1)} %add_rsqrt_fusion) | copy-start | bytes 9028
  102.6 8.0 %copy-start.19 = (bf16[752,512]{1,0:T(8,128)(2,1)S(1)}, bf16[752,512]{1,0:T(8,128)(2,1)}, u32[]{:S(2)}) copy-start(bf16[752,512]{1,0:T(8,128)(2,1)} %copy-done.18) | copy-start | bytes 2310148
  102.6 8.0 %copy-start.84 = (bf16[2048,512]{1,0:T(8,128)(2,1)S(1)}, bf16[2048,512]{1,0:T(8,128)(2,1)}, u32[]{:S(2)}) copy-start(bf16[2048,512]{1,0:T(8,128)(2,1)} %param.41) | copy-start | bytes 6291460
  122.5 117.4 %copy-start.6 = (f32[752,512]{1,0:T(8,128)}, f32[752,512]{1,0:T(8,128)S(1)}, u32[]{:S(2)}) copy-start(f32[752,512]{1,0:T(8,128)S(1)} %get-tuple-element.80) | copy-start | bytes 4620292
  219.8 28.6 %collective-permute-start.9 = (f32[752,1024]{1,0:T(8,128)S(1)}, f32[752,1024]{1,0:T(8,128)S(1)}, u32[]{:S(2)}, u32[]{:S(2)}) collective-permute-start(f32[752,1024]{1,0:T(8,128)S(1)} %pad_maximum_fusion), channel_id=1, source_target_pairs={{1,0},{0,1},{3,2},{2,3},{5,4},{4,5},{7,6},{6,7},{9,8},{8,9},{11,10... | collective-permute-start | bytes 9240584 | tf_op jit(solution)/shard_map/ppermute | solution.py:253
  221.5 6.4 %copy-start.10 = (bf16[1504,512]{0,1:T(8,128)(2,1)S(1)}, bf16[1504,512]{0,1:T(8,128)(2,1)}, u32[]{:S(2)}) copy-start(bf16[1504,512]{0,1:T(8,128)(2,1)} %copy.62) | copy-start | bytes 4620292
  223.3 52.1 %collective-permute-start.5 = (bf16[376,512]{1,0:T(8,128)(2,1)S(1)}, bf16[376,512]{1,0:T(8,128)(2,1)}, u32[]{:S(2)}, u32[]{:S(2)}) collective-permute-start(bf16[376,512]{1,0:T(8,128)(2,1)S(1)} %get-tuple-element.97), channel_id=1, source_target_pairs={{0,0},{2,1},{1,2},{3,3},{4,4},{6,5},{5,6},{7,7},{8,8},{10,9},{9,10... | collective-permute-start | bytes 1155080 | tf_op jit(solution)/shard_map/ppermute | solution.py:147
  224.7 13.1 %copy-start.35 = (bf16[752,512]{1,0:T(8,128)(2,1)S(1)}, bf16[752,512]{1,0:T(8,128)(2,1)}, u32[]{:S(2)}) copy-start(bf16[752,512]{1,0:T(8,128)(2,1)} %copy-done.34) | copy-start | bytes 2310148
  224.7 51.9 %collective-permute-start.6 = (bf16[376,512]{1,0:T(8,128)(2,1)S(1)}, bf16[376,512]{1,0:T(8,128)(2,1)}, u32[]{:S(2)}, u32[]{:S(2)}) collective-permute-start(bf16[376,512]{1,0:T(8,128)(2,1)S(1)} %get-tuple-element.96), channel_id=1, source_target_pairs={{2,0},{0,1},{3,2},{1,3},{6,4},{4,5},{7,6},{5,7},{10,8},{8,9},{11,1... | collective-permute-start | bytes 1155080 | tf_op jit(solution)/shard_map/ppermute | solution.py:147
  249.5 14.7 %copy-start.11 = (bf16[752,1024]{1,0:T(8,128)(2,1)}, bf16[752,1024]{1,0:T(8,128)(2,1)S(1)}, u32[]{:S(2)}) copy-start(bf16[752,1024]{1,0:T(8,128)(2,1)S(1)} %fusion.15) | copy-start | bytes 4620292
  259.5 6.1 %copy-start.69 = (bf16[768]{0:T(1024)(128)(2,1)S(1)}, bf16[768]{0:T(1024)(128)(2,1)}, u32[]{:S(2)}) copy-start(bf16[768]{0:T(1024)(128)(2,1)} %pad.11.clone) | copy-start | bytes 4612
  259.6 6.1 %collective-permute-start.10 = (bf16[1,512]{1,0:T(2,128)(2,1)S(1)}, bf16[1,512]{1,0:T(2,128)(2,1)S(1)}, u32[]{:S(2)}, u32[]{:S(2)}) collective-permute-start(bf16[1,512]{1,0:T(2,128)(2,1)S(1)} %get-tuple-element.93), channel_id=1, source_target_pairs={{1,0},{3,2},{5,4},{7,6},{9,8},{11,10},{13,12},{15,14},{17,16},{19,... | collective-permute-start | bytes 3080 | tf_op jit(solution)/shard_map/ppermute | solution.py:156
  261.0 4.7 collective-permute-start.11
  268.3 4.8 %copy-start.72 = (bf16[14,160]{1,0:T(8,128)(2,1)S(1)}, bf16[14,160]{1,0:T(8,128)(2,1)}, u32[]{:S(2)}) copy-start(bf16[14,160]{1,0:T(8,128)(2,1)} %copy-done.71) | copy-start | bytes 13444
  268.3 4.8 %copy-start.93 = (bf16[1,160]{1,0:T(2,128)(2,1)S(1)}, bf16[1,160]{1,0:T(2,128)(2,1)}, u32[]{:S(2)}) copy-start(bf16[1,160]{1,0:T(2,128)(2,1)} %copy-done.92) | copy-start | bytes 964
  268.3 4.8 %copy-start.95 = (bf16[1,160]{1,0:T(2,128)(2,1)S(1)}, bf16[1,160]{1,0:T(2,128)(2,1)}, u32[]{:S(2)}) copy-start(bf16[1,160]{1,0:T(2,128)(2,1)} %copy-done.94) | copy-start | bytes 964
  268.3 4.8 %copy-start.97 = (bf16[1,80]{1,0:T(2,128)(2,1)S(1)}, bf16[1,80]{1,0:T(2,128)(2,1)}, u32[]{:S(2)}) copy-start(bf16[1,80]{1,0:T(2,128)(2,1)} %copy-done.96) | copy-start | bytes 484
  268.3 4.8 %copy-start.99 = (bf16[1,80]{1,0:T(2,128)(2,1)S(1)}, bf16[1,80]{1,0:T(2,128)(2,1)}, u32[]{:S(2)}) copy-start(bf16[1,80]{1,0:T(2,128)(2,1)} %copy-done.98) | copy-start | bytes 484
  280.7 56.9 %collective-permute-start.12 = (f32[376,160]{0,1:T(8,128)S(1)}, f32[376,160]{0,1:T(8,128)S(1)}, u32[]{:S(2)}, u32[]{:S(2)}) collective-permute-start(f32[376,160]{0,1:T(8,128)S(1)} %get-tuple-element.99), channel_id=1, source_target_pairs={{0,0},{2,1},{1,2},{3,3},{4,4},{6,5},{5,6},{7,7},{8,8},{10,9},{9,10... | collective-permute-start | bytes 721928 | tf_op jit(solution)/shard_map/ppermute | solution.py:147
  281.5 56.3 %collective-permute-start.13 = (f32[376,160]{0,1:T(8,128)S(1)}, f32[376,160]{0,1:T(8,128)S(1)}, u32[]{:S(2)}, u32[]{:S(2)}) collective-permute-start(f32[376,160]{0,1:T(8,128)S(1)} %get-tuple-element.98), channel_id=1, source_target_pairs={{2,0},{0,1},{3,2},{1,3},{6,4},{4,5},{7,6},{5,7},{10,8},{8,9},{11,1... | collective-permute-start | bytes 721928 | tf_op jit(solution)/shard_map/ppermute | solution.py:147
  (70 other events, 173.3 us)
Sparse Core Ops, SparseCore 0:
  275.4 178.6 all-reduce.5

commit v2 on v1

--- a/solution.py
+++ b/solution.py
@@ -1,8 +1,11 @@
+import functools
 import math
 
 import jax
 import jax.numpy as jnp
 from jax import lax
+from jax.experimental import pallas as pl
+from jax.experimental.pallas import tpu as pltpu
 from jax.sharding import PartitionSpec as P
 
 HEADS = 8
@@ -86,6 +89,89 @@
     sb, cb = jnp.sin(b)[None, :, :], jnp.cos(b)[None, :, :]
     both = jnp.concatenate([sa * cb + ca * sb, ca * cb - sa * sb], axis=2)
     return both.reshape(count, width)
+
+
+def half_mask(shape, h, hd):
+    lane = lax.broadcasted_iota(jnp.int32, shape, 1)
+    return (lane >= h*hd) & (lane < (h+1)*hd)
+
+def fwd_kernel(scale, hd, q_ref, k_ref, v_ref, p_ref, o_ref, s_ref):
+    per = 128//hd
+    k = k_ref[...]
+    vt = v_ref[...].T
+    outs=[]
+    for h in range(per):
+        q = q_ref[...]
+        q = jnp.where(half_mask(q.shape,h,hd), q, jnp.zeros_like(q))
+        s_ref[h] = lax.dot_general(k, q, (((1,),(1,)),((),())), preferred_element_type=F32)
+    for h in range(per):
+        s = s_ref[h]
+        m = jnp.max(s, axis=0, keepdims=True)
+        e = jnp.exp((s - m)*scale)
+        l = jnp.sum(e, axis=0, keepdims=True)
+        p = (e * (1.0/l)).astype(BF16)
+        p_ref[h] = p
+        outs.append(jnp.dot(vt[h*hd:(h+1)*hd], p, preferred_element_type=F32))
+    o_ref[...] = jnp.concatenate(outs, axis=0).T
+
+def attn_fwd(q, k, v, scale, heads, QB):
+    R, D = q.shape; N = k.shape[0]; hd = D//heads; per=128//hd; pairs=D//128
+    return pl.pallas_call(
+        functools.partial(fwd_kernel, scale, hd),
+        grid=(pairs, R//QB),
+        in_specs=[pl.BlockSpec((QB,128),lambda p,i:(i,p)),
+                  pl.BlockSpec((N,128),lambda p,i:(0,p)),
+                  pl.BlockSpec((N,128),lambda p,i:(0,p))],
+        out_specs=[pl.BlockSpec((per,N,QB),lambda p,i:(p,0,i)),
+                   pl.BlockSpec((QB,128),lambda p,i:(i,p))],
+        out_shape=[jax.ShapeDtypeStruct((heads,N,R),BF16), jax.ShapeDtypeStruct((R,D),F32)],
+        scratch_shapes=[pltpu.VMEM((per,N,QB),F32)],
+        compiler_params=pltpu.CompilerParams(vmem_limit_bytes=60<<20),
+    )(q,k,v)
+
+def bwd_kernel(scale, hd, q_ref, do_ref, o_ref, k_ref, v_ref, p_ref, dq_ref, dk_ref, dv_ref, dp_ref, kt_ref):
+    per = 128//hd
+    i = pl.program_id(1)
+    @pl.when(i==0)
+    def _():
+        kt_ref[...] = k_ref[...].T
+        dk_ref[...] = jnp.zeros_like(dk_ref)
+        dv_ref[...] = jnp.zeros_like(dv_ref)
+    do = do_ref[...]
+    q = q_ref[...]
+    v = v_ref[...]
+    prod = (do.astype(F32)*o_ref[...]).T
+    for h in range(per):
+        doh = jnp.where(half_mask(do.shape,h,hd), do, jnp.zeros_like(do))
+        dp_ref[h] = lax.dot_general(v, doh, (((1,),(1,)),((),())), preferred_element_type=F32)
+    dqs=[]
+    for h in range(per):
+        doh = jnp.where(half_mask(do.shape,h,hd), do, jnp.zeros_like(do))
+        qh = jnp.where(half_mask(q.shape,h,hd), q, jnp.zeros_like(q))
+        delta = jnp.sum(prod[h*hd:(h+1)*hd], axis=0, keepdims=True)
+        p = p_ref[h]
+        ds = (p.astype(F32)*(dp_ref[h]-delta)).astype(BF16)
+        dv_ref[...] += jnp.dot(p, doh, preferred_element_type=F32)
+        dk_ref[...] += jnp.dot(ds, qh, preferred_element_type=F32)
+        dqs.append(jnp.dot(kt_ref[h*hd:(h+1)*hd], ds, preferred_element_type=F32))
+    dq_ref[...] = (jnp.concatenate(dqs,axis=0)*scale).T.astype(BF16)
+    @pl.when(i==pl.num_programs(1)-1)
+    def _():
+        dk_ref[...] = dk_ref[...]*scale
+
+def attn_bwd(q, do, o, k, v, p, scale, heads, QB):
+    R, D = q.shape; N = k.shape[0]; hd = D//heads; per=128//hd; pairs=D//128
+    row = pl.BlockSpec((QB,128),lambda p,i:(i,p))
+    key = pl.BlockSpec((N,128),lambda p,i:(0,p))
+    return pl.pallas_call(
+        functools.partial(bwd_kernel, scale, hd),
+        grid=(pairs, R//QB),
+        in_specs=[row,row,row,key,key,pl.BlockSpec((per,N,QB),lambda p,i:(p,0,i))],
+        out_specs=[row,key,key],
+        out_shape=[jax.ShapeDtypeStruct((R,D),BF16), jax.ShapeDtypeStruct((N,D),F32), jax.ShapeDtypeStruct((N,D),F32)],
+        scratch_shapes=[pltpu.VMEM((per,N,QB),F32), pltpu.VMEM((128,N),BF16)],
+        compiler_params=pltpu.CompilerParams(vmem_limit_bytes=60<<20),
+    )(q,do,o,k,v,p)
 
 
 def on_device(
@@ -196,15 +282,11 @@
         others.append(lax.ppermute(keyval, "frame", perm))
     whole = jnp.concatenate([keyval] + others, axis=0)
     tokens = whole.shape[0]
-    kh = whole[:, :D].reshape(tokens, HEADS, hd)
-    vh = whole[:, D:].reshape(tokens, HEADS, hd)
-    qh = query.reshape(T, HEADS, hd)
-    scores = jnp.einsum("qhd,khd->hqk", qh, kh, preferred_element_type=F32) * scale
-    exponent = jnp.exp(scores - jnp.max(scores, axis=-1, keepdims=True))
-    probs = exponent / jnp.sum(exponent, axis=-1, keepdims=True)
-    weights = probs.astype(BF16)
-    attended = jnp.einsum("hqk,khd->qhd", weights, vh, preferred_element_type=F32)
-    attended = attended.reshape(T, D).astype(BF16)
+    key_all, value_all = whole[:, :D], whole[:, D:]
+    query_ext = jnp.pad(query, ((0, R - T), (0, 0)))
+    block = 256 if R % 256 == 0 else 128
+    probs, attended_wide = attn_fwd(query_ext, key_all, value_all, scale, HEADS, block)
+    attended = attended_wide[:T].astype(BF16)
     mixed = stream + dot(attended, output_weight) + output_bias
     xhat2, r2 = norm_parts(mixed)
     second_normed = (xhat2 * second_gain + second_shift).astype(BF16)
@@ -238,15 +320,12 @@
         ("dp", "frame"),
     )
 
-    attended_grad = dot_t(branch_grad, output_weight).astype(BF16).reshape(T, HEADS, hd)
-    weight_grad = jnp.einsum("qhd,khd->hqk", attended_grad, vh, preferred_element_type=F32)
-    delta = jnp.sum(weight_grad * probs, axis=-1, keepdims=True)
-    score_grad = (probs * (weight_grad - delta)).astype(BF16)
-    query_grad = jnp.einsum("hqk,khd->qhd", score_grad, kh, preferred_element_type=F32) * scale
-    query_grad = query_grad.astype(BF16).reshape(T, D)
-    key_term = jnp.einsum("hqk,qhd->khd", score_grad, qh, preferred_element_type=F32) * scale
-    value_term = jnp.einsum("hqk,qhd->khd", weights, attended_grad, preferred_element_type=F32)
-    terms = jnp.concatenate([key_term.reshape(tokens, D), value_term.reshape(tokens, D)], axis=1)
+    attended_grad = jnp.pad(dot_t(branch_grad, output_weight).astype(BF16), ((0, R - T), (0, 0)))
+    query_grad, key_term, value_term = attn_bwd(
+        query_ext, attended_grad, attended_wide, key_all, value_all, probs, scale, HEADS, block
+    )
+    query_grad = query_grad[:T]
+    terms = jnp.concatenate([key_term, value_term], axis=1)
     total = terms[:T]
     for t in range(1, G):
         perm = [((i // G) * G + (i % G + t) % G, i) for i in range(F)]

time: 483 us -> 401 us (0.83)
  matrix products: 162 us -> 63.4 us
  Pallas kernels: 0 us -> 49.5 us
  other arithmetic: 58.1 us -> 26.9 us
  local copies, waits for them, and re-layouts: 40 us -> 34.2 us
    dot_general x5 -> x0, matrix products: 79.6 us -> none  [the longest x1 27.8 us: on_device(): jnp.einsum('qhd,khd->hqk', attended_grad, vh, preferred_element_type=F32)]
    pallas_call x0 -> x2, Pallas kernels: none -> 49.5 us  [the longest x1 25.7 us: attn_bwd(): pl.pallas_call(functools.partial(bwd_kernel, scale, hd), grid=(pairs, R /...]
    convert_element_type x1 -> x0, other arithmetic: 30.1 us -> none  [on_device(): score_grad = (probs * (weight_grad - delta)).astype(BF16)]
    sub x1 -> x0, matrix products: 18.2 us -> none  [on_device(): exponent = jnp.exp(scores - jnp.max(scores, axis=-1, keepdims=True))]
    reshape x2 -> x0, local copies, waits for them, and re-layouts: 7.08 us -> none  [the longest x1 3.58 us: on_device(): key_term.reshape(tokens, D)]
    unnamed x217 -> x152, local copies, waits for them, and re-layouts: 10.9 us -> 16.8 us
where the time goes in v2:
time: 401 us; the launch traced here: 394 us
  waiting for transfers between devices  123 us (31%)
  matrix products  63.4 us (16%)
  blocking collectives  52.4 us (13%)
  Pallas kernels  49.5 us (12%)
  local copies, waits for them, and re-layouts  34.2 us (9%)
  starting transfers between devices  28.2 us (7%)
  other arithmetic  26.9 us (7%)
  between operations  16.3 us (4%)
    psum x1, waiting for transfers between devices, on_device(): lax.psum((reduce_matrix_grad.astype(BF16), query_weight_grad.astype(BF16)...  116 us
    psum x1, blocking collectives, on_device(): lax.psum(jnp.concatenate(small).reshape(-1, 128), ('dp', 'frame'))  52.4 us
    dot_general x8, matrix products, dot(): return jnp.dot(left, right, preferred_element_type=F32)  27.8 us
    pallas_call x1, Pallas kernels, attn_bwd(): pl.pallas_call(functools.partial(bwd_kernel, scale, hd), grid=(pairs, R /...  25.7 us
    pallas_call x1, Pallas kernels, attn_fwd(): pl.pallas_call(functools.partial(fwd_kernel, scale, hd), grid=(pairs, R /...  23.8 us
    dot_general x9, matrix products, dot_t(): lax.dot_general(left, right, (((1,), (1,)), ((), ())), preferred_element_...  19.5 us
    unnamed x152, local copies, waits for them, and re-layouts  16.8 us
    dot_general x8, matrix products, outer(): lax.dot_general(left, right, (((0,), (0,)), ((), ())), preferred_element_...  16.1 us
  transfers between devices with their start and end apart: 15, of which 4 were waited for; matrix products, arithmetic and copies ran while one was open for 13% of the time, Pallas kernels for 0%

profile of v2, /device:TPU:0, one launch (start us, length us, event | category | flops | bytes accessed | tf_op | source)
XLA Modules:
  0.0 393.6 jit_solution(15791149278204137297)
XLA Ops:
  7.3 1.3 copy.43
  8.9 1.3 collective-permute-start
  10.2 3.6 collective-permute-start.1
  16.4 2.0 collective-permute-done.1
  18.4 2.8 collective-permute-start.2
  21.2 1.3 collective-permute-start.3
  22.6 1.6 collective-permute-done.3
  24.2 6.2 %select_convert_fusion.1 = (bf16[768,1024]{1,0:T(8,128)(2,1)S(1)}, f32[768,1024]{1,0:T(8,128)}) fusion(f32[1024]{0:T(1024)S(1)} %pad_maximum_fusion.14, pred[768]{0:T(1024)(128)(4,1)S(1)} %fusion.79, bf16[240,512]{1,0:T(8,128)(2,1)} %bitcast.86, bf16[1,160]{1,0:T(2,128)(2,1)S(1)} %collective-permute-done.2, bf16[14,160]{1,0:T(8,128)(2,1)S(1)} %broadcast_in_dim.36, ...), kind=kOutput, calls=%fused_computation.14 | convolution fusion | flops 531988480 | bytes 5215296 | tf_op jit(solution)/shard_map/dot_general | solution.py:49
  30.7 2.0 copy-done.38
  32.9 3.9 fusion.95
  40.3 1.4 pad_maximum_fusion.2
  42.9 4.6 %collective-permute-start.7 = (bf16[376,512]{1,0:T(8,128)(2,1)}, bf16[376,512]{1,0:T(8,128)(2,1)}, u32[]{:S(2)}, u32[]{:S(2)}) collective-permute-start(bf16[376,512]{1,0:T(8,128)(2,1)} %get-tuple-element.84), channel_id=1, source_target_pairs={{0,0},{1,2},{2,1},{3,3},{4,4},{5,6},{6,5},{7,7},{8,8},{9,10},{10,9... | collective-permute-start | bytes 1155080 | tf_op jit(solution)/shard_map/ppermute | solution.py:221
  48.2 1.7 add_convert_fusion.2
  52.0 3.4 collective-permute-done.8
  57.3 1.7 pad_maximum_fusion
  59.0 2.0 fusion.96
  61.0 23.8 %shard_map.373 = (bf16[8,1504,768]{2,1,0:T(8,128)(2,1)}, f32[768,512]{1,0:T(8,128)}) custom-call(bf16[768,512]{1,0:T(8,128)(2,1)} %pad.10.q_ref, bf16[1504,512]{1,0:T(8,128)(2,1)} %get-tuple-element.75.k_ref, bf16[1504,512]{1,0:T(8,128)(2,1)} %get-tuple-element.74.v_ref), custom_call_target="tpu_custom_call" | custom-call | tf_op jit(solution)/shard_map/pallas_call | solution.py:119
  84.8 2.2 fusion.101
  87.8 8.0 %multiply_convert_fusion.1 = (bf16[752,2048]{1,0:T(8,128)(2,1)}, f32[752,2048]{1,0:T(8,128)S(1)}) fusion(f32[2048]{0:T(1024)S(1)} %copy-done.61, bf16[512,2048]{1,0:T(8,128)(2,1)S(1)} %copy-done, f32[752,512]{1,0:T(8,128)S(1)} %get-tuple-element.113, f32[512]{0:T(512)S(1)} %copy-done.54, f32[512]{0:T(512)S(1)} %copy-done.53, f32[752]{0:T(1024)S(1)} %add_rsqrt_fusion, ...), kind=kOutput, calls=%fused_computation.5 | convolution fusion | flops 1615945728 | bytes 12896128 | tf_op jit(solution)/shard_map/dot_general | solution.py:49
  95.7 7.0 %convert_reduce_fusion = (f32[2048]{0:T(1024)S(1)}, bf16[752,2048]{1,0:T(8,128)(2,1)S(1)}) fusion(bf16[2048,512]{1,0:T(8,128)(2,1)S(1)} %copy-done.59, bf16[752,512]{1,0:T(8,128)(2,1)S(1)} %copy-done.16, pred[]{:T(512)S(6)} %lt.84, f32[752,2048]{1,0:T(8,128)S(1)} %get-tuple-element.115, f32[2048]{0:T(1024)S(1)} %copy-done.61), kind=kOutput, calls=%fused_computation.3 | convolution fusion | flops 1622104064 | bytes 12124161 | tf_op jit(solution)/shard_map/dot_general | solution.py:53
  102.8 2.2 multiply_reduce_fusion
  107.6 25.7 %shard_map.374 = (bf16[768,512]{1,0:T(8,128)(2,1)}, f32[1504,512]{1,0:T(8,128)}, f32[1504,512]{1,0:T(8,128)}) custom-call(bf16[768,512]{1,0:T(8,128)(2,1)} %pad.10.q_ref, bf16[768,512]{1,0:T(8,128)(2,1)} %pad.11.do_ref, f32[768,512]{1,0:T(8,128)} %get-tuple-element.26.o_ref, bf16[1504,512]{1,0:T(8,128)(2,1)} %get-tuple-element.75.k_ref, ...), custom_call_target="tpu_custom_call" | custom-call | tf_op jit(solution)/shard_map/pallas_call | solution.py:166
  133.3 2.3 constant_dynamic-update-slice_fusion.1
  136.6 1.9 slice.282
  138.4 1.7 copy-done.9
  142.4 4.8 %select_convert_fusion.2 = bf16[752,512]{1,0:T(8,128)(2,1)S(1)} fusion(f32[752,512]{1,0:T(8,128)} %copy-done.7, bf16[752,2048]{1,0:T(8,128)(2,1)} %get-tuple-element.114, bf16[2048,512]{1,0:T(8,128)(2,1)} %param.41, f32[512]{0:T(512)S(1)} %copy-done.65, pred[]{:T(512)S(6)} %lt.84), kind=kOutput, calls=%fused_computation.46 | convolution fusion | flops 1578598400 | bytes 7489537 | tf_op jit(solution)/shard_map/dot_general | solution.py:49
  148.0 4.6 %collective-permute-start.5 = (bf16[376,512]{1,0:T(8,128)(2,1)}, bf16[376,512]{1,0:T(8,128)(2,1)}, u32[]{:S(2)}, u32[]{:S(2)}) collective-permute-start(bf16[376,512]{1,0:T(8,128)(2,1)} %get-tuple-element.86), channel_id=1, source_target_pairs={{0,0},{2,1},{1,2},{3,3},{4,4},{6,5},{5,6},{7,7},{8,8},{10,9},{9,10... | collective-permute-start | bytes 1155080 | tf_op jit(solution)/shard_map/ppermute | solution.py:233
  152.6 1.4 convolution_convert_fusion.8
  155.4 1.4 convolution_convert_fusion.5
  156.8 3.2 convolution_convert_fusion
  160.0 3.4 convolution_convert_fusion.1
  163.4 2.4 fusion.2
  166.5 1.3 copy-done.4
  169.8 2.0 convert_reduce_fusion.6
  171.9 2.6 convolution_convert_fusion.2
  174.5 1.4 convolution_convert_fusion.6
  175.9 1.3 collective-permute-start.10
  177.2 3.7 collective-permute-start.11
  180.9 1.4 convolution_convert_fusion.7
  182.8 1.8 fusion.11
  184.9 4.7 %select_convert_fusion = bf16[768,1024]{1,0:T(8,128)(2,1)S(1)} fusion(f32[768,512]{1,0:T(8,128)S(1)} %fusion.11, f32[768,1024]{1,0:T(8,128)S(1)} %copy-done.67, bf16[1024,512]{1,0:T(8,128)(2,1)S(1)} %bitcast.78, f32[1024]{0:T(1024)S(1)} %pad_maximum_fusion.14, pred[768]{0:T(1024)(128)(4,1)S(1)} %fusion.79, bf16[1,512]{1,0:T(2,128)(2,1)S(1)} %collective-permute-done.11, ...), kind=kOutput, calls=%fused_computation.13 | convolution fusion | flops 831258624 | bytes 8118528 | tf_op jit(solution)/shard_map/dot_general | solution.py:53
  189.7 1.3 fusion.5
  197.6 3.0 collective-permute-start.13
  201.0 52.4 %psum.64 = f32[56,128]{1,0:T(8,128)S(1)} all-reduce(f32[56,128]{1,0:T(8,128)S(1)} %bitcast.85), channel_id=1, replica_groups=mesh['dp'=8,'frame'=4] {'dp','frame'}, use_global_device_ids=true, to_apply=%region_20.21 | all-reduce | flops 7168 | bytes 57344 | tf_op jit(solution)/shard_map/psum | solution.py:399
  256.3 115.7 %all-reduce.8.cloned.1.call-done = (bf16[3,80,512]{2,1,0:T(8,128)(2,1)}, bf16[3,512,512]{2,1,0:T(8,128)(2,1)}, bf16[512,512]{1,0:T(8,128)(2,1)}, bf16[512,512]{1...) async-done(((bf16[3,80,512]{2,1,0:T(8,128)(2,1)}, ...) | async-done | bytes 8110096 | tf_op jit(solution)/shard_map/psum | solution.py:375
  372.1 4.3 %convert_element_type.164 = f32[512,2048]{1,0:T(8,128)} convert(bf16[512,2048]{1,0:T(8,128)(2,1)} %get-tuple-element.66) | non-fusion elementwise | flops 1048576 | bytes 6291456 | tf_op jit(solution)/shard_map/convert_element_type | solution.py:405
  376.3 2.6 convert_element_type.166
  379.0 2.1 reshape.297
  (246 shorter events, 39.1 us)
Async XLA Ops:
  7.2 80.2 %copy-start = (bf16[512,2048]{1,0:T(8,128)(2,1)S(1)}, bf16[512,2048]{1,0:T(8,128)(2,1)}, u32[]{:S(2)}) copy-start(bf16[512,2048]{1,0:T(8,128)(2,1)} %param.39) | copy-start | bytes 6291460
  7.2 364.9 %all-reduce.8.cloned.1.call-start = ((), (), s32[]{:S(2)}) async-start(), calls=%async_computation | async-start | bytes 16220160 | tf_op jit(solution)/shard_map/psum | solution.py:375
  8.6 6.7 %copy-start.58 = (f32[512]{0:T(512)S(1)}, f32[512]{0:T(512)}, u32[]{:S(2)}) copy-start(f32[512]{0:T(512)} %param.25) | copy-start | bytes 6148
  8.9 6.5 %collective-permute-start = (bf16[376,160]{1,0:T(8,128)(2,1)S(1)}, bf16[376,160]{1,0:T(8,128)(2,1)}, u32[]{:S(2)}, u32[]{:S(2)}) collective-permute-start(bf16[376,160]{1,0:T(8,128)(2,1)S(1)} %get-tuple-element.92), channel_id=1, source_target_pairs={{0,0},{1,2},{2,1},{3,3},{4,4},{5,6},{6,5},{7,7},{8,8},{9,10},{10,9... | collective-permute-start | bytes 360968 | tf_op jit(solution)/shard_map/ppermute | solution.py:221
  10.2 8.2 %collective-permute-start.1 = (bf16[376,160]{1,0:T(8,128)(2,1)S(1)}, bf16[376,160]{1,0:T(8,128)(2,1)S(1)}, u32[]{:S(2)}, u32[]{:S(2)}) collective-permute-start(bf16[376,160]{1,0:T(8,128)(2,1)S(1)} %get-tuple-element.91), channel_id=1, source_target_pairs={{0,2},{1,0},{2,3},{3,1},{4,6},{5,4},{6,7},{7,5},{8,10},{9,8},{10,1... | collective-permute-start | bytes 360968 | tf_op jit(solution)/shard_map/ppermute | solution.py:221
  18.4 12.1 %copy-start.50 = (bf16[752,160]{1,0:T(8,128)(2,1)}, bf16[752,160]{1,0:T(8,128)(2,1)S(1)}, u32[]{:S(2)}) copy-start(bf16[752,160]{1,0:T(8,128)(2,1)S(1)} %constant_dynamic-update-slice_fusion.17) | copy-start | bytes 721924
  18.4 4.1 %collective-permute-start.2 = (bf16[1,160]{1,0:T(2,128)(2,1)S(1)}, bf16[1,160]{1,0:T(2,128)(2,1)S(1)}, u32[]{:S(2)}, u32[]{:S(2)}) collective-permute-start(bf16[1,160]{1,0:T(2,128)(2,1)S(1)} %get-tuple-element.90), channel_id=1, source_target_pairs={{0,1},{2,3},{4,5},{6,7},{8,9},{10,11},{12,13},{14,15},{16,17},{18,... | collective-permute-start | bytes 968 | tf_op jit(solution)/shard_map/ppermute | solution.py:241
  21.2 3.1 collective-permute-start.3
  30.6 6.2 %copy-start.26 = (bf16[752,1024]{1,0:T(8,128)(2,1)}, bf16[752,1024]{1,0:T(8,128)(2,1)S(1)}, u32[]{:S(2)}) copy-start(bf16[752,1024]{1,0:T(8,128)(2,1)S(1)} %slice.277) | copy-start | bytes 4620292
  30.7 6.1 %copy-start.31 = (bf16[767,512]{1,0:T(8,128)(2,1)}, bf16[767,512]{1,0:T(8,128)(2,1)S(1)}, u32[]{:S(2)}) copy-start(bf16[767,512]{1,0:T(8,128)(2,1)S(1)} %slice.276) | copy-start | bytes 2356228
  40.3 2.6 copy-start.13
  41.7 6.5 %copy-start.46 = (bf16[512,512]{1,0:T(8,128)(2,1)S(1)}, bf16[512,512]{1,0:T(8,128)(2,1)}, u32[]{:S(2)}) copy-start(bf16[512,512]{1,0:T(8,128)(2,1)} %param.30) | copy-start | bytes 1572868
  41.7 6.5 %copy-start.64 = (f32[512]{0:T(512)S(1)}, f32[512]{0:T(512)}, u32[]{:S(2)}) copy-start(f32[512]{0:T(512)} %param.31) | copy-start | bytes 6148
  41.7 15.6 %collective-permute-start.4 = (bf16[752,1024]{1,0:T(8,128)(2,1)}, bf16[752,1024]{1,0:T(8,128)(2,1)}, u32[]{:S(2)}, u32[]{:S(2)}) collective-permute-start(bf16[752,1024]{1,0:T(8,128)(2,1)} %pad_maximum_fusion.2), channel_id=1, source_target_pairs={{0,1},{1,0},{2,3},{3,2},{4,5},{5,4},{6,7},{7,6},{8,9},{9,8},{10,11... | collective-permute-start | bytes 4620296 | tf_op jit(solution)/shard_map/ppermute | solution.py:282
  42.9 7.9 %collective-permute-start.7 = (bf16[376,512]{1,0:T(8,128)(2,1)}, bf16[376,512]{1,0:T(8,128)(2,1)}, u32[]{:S(2)}, u32[]{:S(2)}) collective-permute-start(bf16[376,512]{1,0:T(8,128)(2,1)} %get-tuple-element.84), channel_id=1, source_target_pairs={{0,0},{1,2},{2,1},{3,3},{4,4},{5,6},{6,5},{7,7},{8,8},{9,10},{10,9... | collective-permute-start | bytes 1155080 | tf_op jit(solution)/shard_map/ppermute | solution.py:221
  47.5 7.8 %collective-permute-start.8 = (bf16[376,512]{1,0:T(8,128)(2,1)}, bf16[376,512]{1,0:T(8,128)(2,1)}, u32[]{:S(2)}, u32[]{:S(2)}) collective-permute-start(bf16[376,512]{1,0:T(8,128)(2,1)} %get-tuple-element.83), channel_id=1, source_target_pairs={{0,2},{1,0},{2,3},{3,1},{4,6},{5,4},{6,7},{7,5},{8,10},{9,8},{10,1... | collective-permute-start | bytes 1155080 | tf_op jit(solution)/shard_map/ppermute | solution.py:221
  50.8 6.4 %copy-start.14 = (bf16[752,512]{1,0:T(8,128)(2,1)S(1)}, bf16[752,512]{1,0:T(8,128)(2,1)}, u32[]{:S(2)}) copy-start(bf16[752,512]{1,0:T(8,128)(2,1)} %copy-done.13) | copy-start | bytes 2310148
  61.0 23.8 %copy-start.3 = (f32[752,512]{1,0:T(8,128)S(1)}, f32[752,512]{1,0:T(8,128)}, u32[]{:S(2)}) copy-start(f32[752,512]{1,0:T(8,128)} %copy-done.2) | copy-start | bytes 4620292
  61.0 23.8 %copy-start.57 = (f32[512]{0:T(512)S(1)}, f32[512]{0:T(512)}, u32[]{:S(2)}) copy-start(f32[512]{0:T(512)} %param.36) | copy-start | bytes 6148
  86.9 18.1 %copy-start.7 = (f32[752,512]{1,0:T(8,128)}, f32[752,512]{1,0:T(8,128)S(1)}, u32[]{:S(2)}) copy-start(f32[752,512]{1,0:T(8,128)S(1)} %get-tuple-element.113) | copy-start | bytes 4620292
  87.8 8.0 %copy-start.16 = (bf16[752,512]{1,0:T(8,128)(2,1)S(1)}, bf16[752,512]{1,0:T(8,128)(2,1)}, u32[]{:S(2)}) copy-start(bf16[752,512]{1,0:T(8,128)(2,1)} %copy-done.15) | copy-start | bytes 2310148
  87.8 8.0 %copy-start.59 = (bf16[2048,512]{1,0:T(8,128)(2,1)S(1)}, bf16[2048,512]{1,0:T(8,128)(2,1)}, u32[]{:S(2)}) copy-start(bf16[2048,512]{1,0:T(8,128)(2,1)} %param.41) | copy-start | bytes 6291460
  105.9 48.7 %copy-start.5 = (f32[752,512]{1,0:T(8,128)}, f32[752,512]{1,0:T(8,128)S(1)}, u32[]{:S(2)}) copy-start(f32[752,512]{1,0:T(8,128)S(1)} %get-tuple-element.69) | copy-start | bytes 4620292
  133.3 2.8 copy-start.19
  136.6 3.6 copy-start.9
  136.6 4.7 %copy-start.39 = (bf16[3,512,512]{2,1,0:T(8,128)(2,1)S(1)}, bf16[3,512,512]{2,1,0:T(8,128)(2,1)}, u32[]{:S(2)}) copy-start(bf16[3,512,512]{2,1,0:T(8,128)(2,1)} %param.26) | copy-start | bytes 4718596
  140.1 23.3 %collective-permute-start.9 = (f32[752,1024]{1,0:T(8,128)}, f32[752,1024]{1,0:T(8,128)}, u32[]{:S(2)}, u32[]{:S(2)}) collective-permute-start(f32[752,1024]{1,0:T(8,128)} %slice.282), channel_id=1, source_target_pairs={{1,0},{0,1},{3,2},{2,3},{5,4},{4,5},{7,6},{6,7},{9,8},{8,9},{11,10... | collective-permute-start | bytes 9240584 | tf_op jit(solution)/shard_map/ppermute | solution.py:332
  142.4 10.2 %copy-start.34 = (bf16[752,512]{1,0:T(8,128)(2,1)S(1)}, bf16[752,512]{1,0:T(8,128)(2,1)}, u32[]{:S(2)}) copy-start(bf16[752,512]{1,0:T(8,128)(2,1)} %copy-done.33) | copy-start | bytes 2310148
  147.2 5.4 %copy-start.20 = (bf16[768,512]{1,0:T(8,128)(2,1)S(1)}, bf16[768,512]{1,0:T(8,128)(2,1)}, u32[]{:S(2)}) copy-start(bf16[768,512]{1,0:T(8,128)(2,1)} %get-tuple-element.28) | copy-start | bytes 2359300
  148.0 6.0 %copy-start.47 = (bf16[512,512]{1,0:T(8,128)(2,1)S(1)}, bf16[512,512]{1,0:T(8,128)(2,1)}, u32[]{:S(2)}) copy-start(bf16[512,512]{1,0:T(8,128)(2,1)} %param.30) | copy-start | bytes 1572868
  148.0 45.1 %collective-permute-start.5 = (bf16[376,512]{1,0:T(8,128)(2,1)}, bf16[376,512]{1,0:T(8,128)(2,1)}, u32[]{:S(2)}, u32[]{:S(2)}) collective-permute-start(bf16[376,512]{1,0:T(8,128)(2,1)} %get-tuple-element.86), channel_id=1, source_target_pairs={{0,0},{2,1},{1,2},{3,3},{4,4},{6,5},{5,6},{7,7},{8,8},{10,9},{9,10... | collective-permute-start | bytes 1155080 | tf_op jit(solution)/shard_map/ppermute | solution.py:233
  152.6 41.7 %collective-permute-start.6 = (bf16[376,512]{1,0:T(8,128)(2,1)S(1)}, bf16[376,512]{1,0:T(8,128)(2,1)}, u32[]{:S(2)}, u32[]{:S(2)}) collective-permute-start(bf16[376,512]{1,0:T(8,128)(2,1)S(1)} %get-tuple-element.85), channel_id=1, source_target_pairs={{2,0},{0,1},{3,2},{1,3},{6,4},{4,5},{7,6},{5,7},{10,8},{8,9},{11,1... | collective-permute-start | bytes 1155080 | tf_op jit(solution)/shard_map/ppermute | solution.py:233
  154.0 2.8 copy-start.66
  155.4 8.0 %slice-start = ((s8[6160384]{0:T(1024)(128)(4,1)}), s8[4194304]{0:T(1024)(128)(4,1)S(1)}, s32[]{:S(2)}) async-start(s8[6160384]{0:T(1024)(128)(4,1)} %bitcast.75), calls=%async_computation.1 | async-start | bytes 8388608
  156.8 3.2 copy-start.8
  156.8 3.2 copy-start.18
  156.8 6.6 %slice-start.1 = ((s8[6160384]{0:T(1024)(128)(4,1)}), s8[1966080]{0:T(1024)(128)(4,1)S(1)}, s32[]{:S(2)}) async-start(s8[6160384]{0:T(1024)(128)(4,1)} %bitcast.75), calls=%async_computation.2 | async-start | bytes 3932160
  165.9 15.0 %copy-start.11 = (bf16[752,1024]{1,0:T(8,128)(2,1)}, bf16[752,1024]{1,0:T(8,128)(2,1)S(1)}, u32[]{:S(2)}) copy-start(bf16[752,1024]{1,0:T(8,128)(2,1)S(1)} %fusion.2) | copy-start | bytes 4620292
  175.9 6.4 %collective-permute-start.10 = (bf16[1,512]{1,0:T(2,128)(2,1)S(1)}, bf16[1,512]{1,0:T(2,128)(2,1)S(1)}, u32[]{:S(2)}, u32[]{:S(2)}) collective-permute-start(bf16[1,512]{1,0:T(2,128)(2,1)S(1)} %get-tuple-element.82), channel_id=1, source_target_pairs={{1,0},{3,2},{5,4},{7,6},{9,8},{11,10},{13,12},{15,14},{17,16},{19,... | collective-permute-start | bytes 3080 | tf_op jit(solution)/shard_map/ppermute | solution.py:242
  177.2 5.1 %collective-permute-start.11 = (bf16[1,512]{1,0:T(2,128)(2,1)S(1)}, bf16[1,512]{1,0:T(2,128)(2,1)S(1)}, u32[]{:S(2)}, u32[]{:S(2)}) collective-permute-start(bf16[1,512]{1,0:T(2,128)(2,1)S(1)} %get-tuple-element.81), channel_id=1, source_target_pairs={{0,1},{2,3},{4,5},{6,7},{8,9},{10,11},{12,13},{14,15},{16,17},{18,... | collective-permute-start | bytes 3080 | tf_op jit(solution)/shard_map/ppermute | solution.py:241
  184.9 4.7 %copy-start.51 = (bf16[752,160]{1,0:T(8,128)(2,1)S(1)}, bf16[752,160]{1,0:T(8,128)(2,1)}, u32[]{:S(2)}) copy-start(bf16[752,160]{1,0:T(8,128)(2,1)} %copy-done.50) | copy-start | bytes 721924
  193.1 2.5 copy-start.29
  193.1 2.5 copy-start.60
  196.9 57.7 %collective-permute-start.12 = (f32[376,160]{0,1:T(8,128)S(1)}, f32[376,160]{0,1:T(8,128)S(1)}, u32[]{:S(2)}, u32[]{:S(2)}) collective-permute-start(f32[376,160]{0,1:T(8,128)S(1)} %get-tuple-element.88), channel_id=1, source_target_pairs={{0,0},{2,1},{1,2},{3,3},{4,4},{6,5},{5,6},{7,7},{8,8},{10,9},{9,10... | collective-permute-start | bytes 721928 | tf_op jit(solution)/shard_map/ppermute | solution.py:233
  197.6 57.2 %collective-permute-start.13 = (f32[376,160]{0,1:T(8,128)S(1)}, f32[376,160]{0,1:T(8,128)S(1)}, u32[]{:S(2)}, u32[]{:S(2)}) collective-permute-start(f32[376,160]{0,1:T(8,128)S(1)} %get-tuple-element.87), channel_id=1, source_target_pairs={{2,0},{0,1},{3,2},{1,3},{6,4},{4,5},{7,6},{5,7},{10,8},{8,9},{11,1... | collective-permute-start | bytes 721928 | tf_op jit(solution)/shard_map/ppermute | solution.py:233
  372.1 4.3 %copy-start.22 = (bf16[2048,512]{1,0:T(8,128)(2,1)S(1)}, bf16[2048,512]{1,0:T(8,128)(2,1)}, u32[]{:S(2)}) copy-start(bf16[2048,512]{1,0:T(8,128)(2,1)} %get-tuple-element.67) | copy-start | bytes 6291460
  376.3 2.6 copy-start.24
  383.3 3.0 copy-start.1
  (37 other events, 60.8 us)
Sparse Core Ops, SparseCore 0:
  191.9 180.0 all-reduce.7
